TPU v7x, 256 devices: a whole 4x4x8 slice. The times are simulated.
256 devices in a mesh: au: 8 (over y, z_lo), ia: 32 (over z_hi, x, core).
Axes of the slice: x: 4, y: 4, z: 8 (z_hi: 4, z_lo: 2; z = z_hi * 2 + z_lo), core: 2. Of those that a mesh axis runs over, the one named last changes fastest.
Arguments:
- user_factors: bfloat16 [8192, 256], P(('au', 'ia')), may hold values from -6 to 6
- item_factors: bfloat16 [131072, 256], P(('ia', 'au')), may hold values from -6 to 6
- user_tangent: bfloat16 [8192, 256], P(('au', 'ia')), may hold values from -6 to 6
- item_tangent: bfloat16 [131072, 256], P(('ia', 'au')), may hold values from -6 to 6
- block_mask: int32 [64, 1024], P('au', 'ia'), may hold values from 0 to 1, as said below
Outputs:
- user_product: float32 [8192, 256], P(('au', 'ia'))
- item_product: float32 [131072, 256], P(('ia', 'au'))
Inputs may be any that keep to these rules, and one draw needn't show every extreme that they name: `block_mask`: users are grouped in runs of 32 * 32 and items in runs of 512 * 8; where one user group meets one item group, at most 128 of its 8 x 32 blocks are observed, and in every draw one such meeting has exactly 128.
All inputs are finite; a program needn't handle non-finite values.
Results may differ from a plain program's by a relative error of at most 0.0013.
Values may be sent and summed in bfloat16 or wider, within the bound.
A program may use at most 64 MiB of HBM per device.

v0:
```python
import jax
import jax.numpy as jnp
from jax import lax
from jax.sharding import PartitionSpec as P

batch_blocks = 16


def sent_together(arrays, axis, dim, along):
    widths = [a.shape[along] for a in arrays]
    both = jnp.concatenate(arrays, axis=along)
    filled = lax.all_gather(both, axis, axis=dim, tiled=True)
    return tuple(jnp.split(filled, [sum(widths[:k]) for k in range(1, len(widths))], axis=along))


def split_up(x, dim, size):
    before, after = (x.shape[:dim], x.shape[dim + 1 :])
    return jnp.moveaxis(x.reshape(*before, size, -1, *after), dim, 0)


def sent_and_summed(x, axis, dim):
    tiles = split_up(x, dim, lax.axis_size(axis))
    arrived = lax.all_to_all(tiles, axis, split_axis=0, concat_axis=0, tiled=True)
    return arrived.sum(axis=0)


def region_pass(users, user_tan, items, item_tan, mask_part):
    row_blocks, col_blocks = mask_part.shape
    block_rows = users.shape[0] // row_blocks
    width = users.shape[1]
    user_tiles = users.reshape(row_blocks, block_rows, width)
    utan_tiles = user_tan.reshape(row_blocks, block_rows, width)
    item_tiles = items.reshape(col_blocks, block_rows, width)
    itan_tiles = item_tan.reshape(col_blocks, block_rows, width)
    total = row_blocks * col_blocks
    flat = mask_part.reshape(-1)
    index = jnp.arange(total, dtype=jnp.int32)
    order = jnp.argsort((1 - flat) * total + index)
    live = flat[order].astype(jnp.float32)
    order = jnp.concatenate([order, jnp.zeros((batch_blocks,), jnp.int32)])
    live = jnp.concatenate([live, jnp.zeros((batch_blocks,), jnp.float32)])
    row_ids = order // col_blocks
    col_ids = order % col_blocks
    scaling = 1.0 / jnp.sqrt(jnp.float32(width))
    observed_count = jnp.sum(flat)
    turns = (observed_count + batch_blocks - 1) // batch_blocks

    def one_turn(turn, carry):
        acc_user, acc_item = carry
        first = (turn * batch_blocks).astype(jnp.int32)
        rsel = lax.dynamic_slice_in_dim(row_ids, first, batch_blocks)
        csel = lax.dynamic_slice_in_dim(col_ids, first, batch_blocks)
        lsel = lax.dynamic_slice_in_dim(live, first, batch_blocks)
        urow = user_tiles[rsel]
        durow = utan_tiles[rsel]
        vrow = item_tiles[csel]
        dvrow = itan_tiles[csel]
        score = jnp.einsum("gar,gbr->gab", urow, vrow, preferred_element_type=jnp.float32) * scaling
        prob = jax.nn.sigmoid(score)
        weight = prob * (1.0 - prob)
        tang = (
            jnp.einsum("gar,gbr->gab", durow, vrow, preferred_element_type=jnp.float32)
            + jnp.einsum("gar,gbr->gab", urow, dvrow, preferred_element_type=jnp.float32)
        ) * scaling
        curv = (lsel[:, None, None] * weight * tang).astype(jnp.bfloat16)
        to_user = jnp.einsum("gab,gbr->gar", curv, vrow, preferred_element_type=jnp.float32)
        to_item = jnp.einsum("gab,gar->gbr", curv, urow, preferred_element_type=jnp.float32)
        onehot_rows = (rsel[:, None] == jnp.arange(row_blocks, dtype=jnp.int32)[None, :]).astype(
            jnp.float32
        )
        onehot_cols = (csel[:, None] == jnp.arange(col_blocks, dtype=jnp.int32)[None, :]).astype(
            jnp.float32
        )
        acc_user = acc_user + jnp.einsum(
            "gk,gar->kar", onehot_rows, to_user, precision=lax.Precision.HIGHEST
        )
        acc_item = acc_item + jnp.einsum(
            "gk,gbr->kbr", onehot_cols, to_item, precision=lax.Precision.HIGHEST
        )
        return (acc_user, acc_item)

    start = (
        jnp.zeros((row_blocks, block_rows, width), jnp.float32),
        jnp.zeros((col_blocks, block_rows, width), jnp.float32),
    )
    acc_user, acc_item = lax.fori_loop(0, turns, one_turn, start)
    return ((acc_user * scaling).reshape(-1, width), (acc_item * scaling).reshape(-1, width))


def on_device(user_factors, item_factors, user_tangent, item_tangent, block_mask):
    users, user_tan = (
        lax.all_gather(user_factors, "ia", axis=0, tiled=True),
        lax.all_gather(user_tangent, "ia", axis=0, tiled=True),
    )
    item_product = None
    piece_items, piece_tan = sent_together((item_factors, item_tangent), "au", 0, 1)
    add_user, add_item = region_pass(users, user_tan, piece_items, piece_tan, block_mask)
    item_product = sent_and_summed(add_item, "au", 0)
    user_product = sent_and_summed(add_user, "ia", 0)
    return (user_product, item_product)


def solution(mesh):
    placed = (
        P(("au", "ia"), None),
        P(("ia", "au"), None),
        P(("au", "ia"), None),
        P(("ia", "au"), None),
        P("au", "ia"),
    )
    return jax.shard_map(
        on_device,
        mesh=mesh,
        in_specs=placed,
        out_specs=(P(("au", "ia"), None), P(("ia", "au"), None)),
        check_vma=False,
    )
```

profile of v0, /device:TPU:1, one launch (start us, length us, event | category | flops | bytes accessed | tf_op | source)
XLA Modules:
  0.0 371.0 jit_solution(9530707863878049275)
XLA Ops:
  11.9 3.2 sort.17
  15.1 1.9 gather_fusion.4
  17.1 51.9 %all_gather.9 = bf16[1024,256]{1,0:T(8,128)(2,1)S(1)} all-gather(bf16[32,256]{1,0:T(8,128)(2,1)S(1)} %copy-done.7), channel_id=1, replica_groups=mesh['au'=8,'ia'=32] {'ia'}, dimensions={0}, use_global_device_ids=true | all-gather | bytes 540672 | tf_op jit(solution)/shard_map/all_gather | solution.py:92
  69.0 44.9 %all_gather.11 = bf16[1024,256]{1,0:T(8,128)(2,1)} all-gather(bf16[32,256]{1,0:T(8,128)(2,1)S(1)} %copy-done.8), channel_id=1, replica_groups=mesh['au'=8,'ia'=32] {'ia'}, dimensions={0}, use_global_device_ids=true | all-gather | bytes 540672 | tf_op jit(solution)/shard_map/all_gather | solution.py:93
  113.9 3.0 all-gather.2.cloned.1.call-done
  116.9 4.5 %fusion.22 = (bf16[4096,256]{1,0:T(8,128)(2,1)}, bf16[4096,256]{1,0:T(8,128)(2,1)}) fusion(bf16[4096,512]{1,0:T(8,128)(2,1)} %all-gather.2.cloned.1.call-done), kind=kLoop, calls=%fused_computation.47 | loop fusion | bytes 8388608 | tf_op jit(solution)/shard_map/split | solution.py:13
  122.4 2.5 broadcast_in_dim.11
  124.9 136.2 %while.12 = (s32[]{:T(128)}, f32[8,128,256]{2,0,1:T(8,128)}, f32[32,128,256]{2,0,1:T(8,128)}, s32[]{:T(128)}, s32[272]{0:T(512)S(1)}, /*index=5*/f32[272]{0:T(51...) while((s32[]{:T(128)}, f32[8,128,256]{2,0,1:T(8,128)}, ...), condition=%wide.region_3.4_spmd, body=%wide.region_2.3_spmd.sunk | while | flops 926944000 | bytes 91760072 | solution.py:86
  125.1 2.2 gather_fusion.1
  127.3 3.2 gather_fusion.3
  136.6 2.3 fusion.74
  138.9 3.5 convolution_add_fusion.3
  142.4 1.9 copy-done.1
  144.5 2.2 gather_fusion.1
  146.8 3.2 gather_fusion.3
  156.1 2.3 fusion.74
  158.4 3.5 convolution_add_fusion.3
  164.0 2.2 gather_fusion.1
  166.2 3.2 gather_fusion.3
  175.5 2.3 fusion.74
  177.8 3.5 convolution_add_fusion.3
  183.4 2.2 gather_fusion.1
  185.7 3.2 gather_fusion.3
  195.0 2.3 fusion.74
  197.3 3.5 convolution_add_fusion.3
  200.8 1.9 copy-done.1
  202.9 2.2 gather_fusion.1
  205.1 3.2 gather_fusion.3
  214.4 2.3 fusion.74
  216.8 3.5 convolution_add_fusion.3
  220.3 1.9 copy-done.1
  222.4 2.2 gather_fusion.1
  224.6 3.2 gather_fusion.3
  233.9 2.3 fusion.74
  236.2 3.5 convolution_add_fusion.3
  239.7 1.9 copy-done.1
  241.8 2.2 gather_fusion.1
  244.1 3.2 gather_fusion.3
  253.3 2.3 fusion.74
  255.7 3.5 convolution_add_fusion.3
  259.2 1.9 copy-done.1
  261.1 2.6 copy_multiply_fusion.1
  263.7 19.6 %all-to-all-start = ((f32[32,32,256]{2,1,0:T(8,128)}), f32[32,32,256]{2,1,0:T(8,128)S(1)}, u32[]{:S(2)}, u32[]{:S(2)}) async-start(f32[32,32,256]{2,1,0:T(8,128)} %bitcast.6), calls=%async_computation | async-start | bytes 2097152 | tf_op jit(solution)/shard_map/all_to_all | solution.py:23
  283.3 6.9 %copy_multiply_fusion = f32[32,128,256]{2,1,0:T(8,128)} fusion(f32[32,128,256]{2,0,1:T(8,128)} %get-tuple-element.64), kind=kLoop, calls=%fused_computation.31 | loop fusion | flops 1048576 | bytes 8388608 | tf_op jit(solution)/shard_map/mul | solution.py:87
  290.2 16.8 %all-to-all-done = f32[32,32,256]{2,1,0:T(8,128)S(1)} async-done(((f32[32,32,256]{2,1,0:T(8,128)}), f32[32,32,256]{2,1,0:T(8,128)S(1)}, u32[]{:S(2)}, u32[]{:S(2)}) %all-to-all-start) | async-done | bytes 1048608 | tf_op jit(solution)/shard_map/all_to_all | solution.py:23
  307.0 4.5 %all-to-all-start.1 = ((f32[8,512,256]{2,1,0:T(8,128)}), f32[8,512,256]{2,1,0:T(8,128)}, u32[]{:S(2)}, u32[]{:S(2)}) async-start(f32[8,512,256]{2,1,0:T(8,128)} %bitcast.50), calls=%async_computation.1 | async-start | bytes 8388608 | tf_op jit(solution)/shard_map/all_to_all | solution.py:23
  312.2 48.6 %all-to-all-done.1 = f32[8,512,256]{2,1,0:T(8,128)} async-done(((f32[8,512,256]{2,1,0:T(8,128)}), f32[8,512,256]{2,1,0:T(8,128)}, u32[]{:S(2)}, u32[]{:S(2)}) %all-to-all-start.1) | async-done | bytes 4194336 | tf_op jit(solution)/shard_map/all_to_all | solution.py:23
  360.8 3.3 reduce_sum.29
  (188 shorter events, 53.5 us)
Async XLA Ops:
  7.2 9.9 %copy-start.7 = (bf16[32,256]{1,0:T(8,128)(2,1)S(1)}, bf16[32,256]{1,0:T(8,128)(2,1)}, u32[]{:S(2)}) copy-start(bf16[32,256]{1,0:T(8,128)(2,1)} %param.7) | copy-start | bytes 49156
  7.2 61.8 %copy-start.8 = (bf16[32,256]{1,0:T(8,128)(2,1)S(1)}, bf16[32,256]{1,0:T(8,128)(2,1)}, u32[]{:S(2)}) copy-start(bf16[32,256]{1,0:T(8,128)(2,1)} %param.9) | copy-start | bytes 49156
  7.2 109.7 %all-gather.2.cloned.1.call-start = ((), (), s32[]{:S(2)}) async-start(), calls=%async_computation.2 | async-start | bytes 4718592 | tf_op jit(solution)/shard_map/all_gather | solution.py:12
  124.9 5.6 %copy-start.3 = (bf16[8,128,256]{2,1,0:T(8,128)(2,1)}, bf16[8,128,256]{2,1,0:T(8,128)(2,1)S(1)}, u32[]{:S(2)}) copy-start(bf16[8,128,256]{2,1,0:T(8,128)(2,1)S(1)} %get-tuple-element.209) | copy-start | bytes 1572868 | tf_op jit(solution)/shard_map/while
  133.2 1.2 copy-start.2
  136.6 2.3 copy-start
  138.9 3.5 copy-start.6
  138.9 5.4 %copy-start.4 = (bf16[8,128,256]{2,1,0:T(8,128)(2,1)S(1)}, bf16[8,128,256]{2,1,0:T(8,128)(2,1)}, u32[]{:S(2)}) copy-start(bf16[8,128,256]{2,1,0:T(8,128)(2,1)} %copy-done.3) | copy-start | bytes 1572868 | tf_op jit(solution)/shard_map/while
  142.4 1.9 copy-start.1
  144.4 5.6 %copy-start.3 = (bf16[8,128,256]{2,1,0:T(8,128)(2,1)}, bf16[8,128,256]{2,1,0:T(8,128)(2,1)S(1)}, u32[]{:S(2)}) copy-start(bf16[8,128,256]{2,1,0:T(8,128)(2,1)S(1)} %get-tuple-element.209) | copy-start | bytes 1572868 | tf_op jit(solution)/shard_map/while
  152.7 1.2 copy-start.2
  154.8 1.2 copy-start.5
  156.1 2.3 copy-start
  158.4 3.5 copy-start.6
  158.4 5.4 %copy-start.4 = (bf16[8,128,256]{2,1,0:T(8,128)(2,1)S(1)}, bf16[8,128,256]{2,1,0:T(8,128)(2,1)}, u32[]{:S(2)}) copy-start(bf16[8,128,256]{2,1,0:T(8,128)(2,1)} %copy-done.3) | copy-start | bytes 1572868 | tf_op jit(solution)/shard_map/while
  161.9 1.9 copy-start.1
  163.8 5.6 %copy-start.3 = (bf16[8,128,256]{2,1,0:T(8,128)(2,1)}, bf16[8,128,256]{2,1,0:T(8,128)(2,1)S(1)}, u32[]{:S(2)}) copy-start(bf16[8,128,256]{2,1,0:T(8,128)(2,1)S(1)} %get-tuple-element.209) | copy-start | bytes 1572868 | tf_op jit(solution)/shard_map/while
  172.1 1.2 copy-start.2
  175.5 2.3 copy-start
  177.8 3.5 copy-start.6
  177.8 5.4 %copy-start.4 = (bf16[8,128,256]{2,1,0:T(8,128)(2,1)S(1)}, bf16[8,128,256]{2,1,0:T(8,128)(2,1)}, u32[]{:S(2)}) copy-start(bf16[8,128,256]{2,1,0:T(8,128)(2,1)} %copy-done.3) | copy-start | bytes 1572868 | tf_op jit(solution)/shard_map/while
  181.3 1.9 copy-start.1
  183.3 5.6 %copy-start.3 = (bf16[8,128,256]{2,1,0:T(8,128)(2,1)}, bf16[8,128,256]{2,1,0:T(8,128)(2,1)S(1)}, u32[]{:S(2)}) copy-start(bf16[8,128,256]{2,1,0:T(8,128)(2,1)S(1)} %get-tuple-element.209) | copy-start | bytes 1572868 | tf_op jit(solution)/shard_map/while
  191.6 1.2 copy-start.2
  195.0 2.3 copy-start
  197.3 3.5 copy-start.6
  197.3 5.4 %copy-start.4 = (bf16[8,128,256]{2,1,0:T(8,128)(2,1)S(1)}, bf16[8,128,256]{2,1,0:T(8,128)(2,1)}, u32[]{:S(2)}) copy-start(bf16[8,128,256]{2,1,0:T(8,128)(2,1)} %copy-done.3) | copy-start | bytes 1572868 | tf_op jit(solution)/shard_map/while
  200.8 1.9 copy-start.1
  202.7 5.6 %copy-start.3 = (bf16[8,128,256]{2,1,0:T(8,128)(2,1)}, bf16[8,128,256]{2,1,0:T(8,128)(2,1)S(1)}, u32[]{:S(2)}) copy-start(bf16[8,128,256]{2,1,0:T(8,128)(2,1)S(1)} %get-tuple-element.209) | copy-start | bytes 1572868 | tf_op jit(solution)/shard_map/while
  211.0 1.2 copy-start.2
  214.4 2.3 copy-start
  216.7 3.5 copy-start.6
  216.8 5.4 %copy-start.4 = (bf16[8,128,256]{2,1,0:T(8,128)(2,1)S(1)}, bf16[8,128,256]{2,1,0:T(8,128)(2,1)}, u32[]{:S(2)}) copy-start(bf16[8,128,256]{2,1,0:T(8,128)(2,1)} %copy-done.3) | copy-start | bytes 1572868 | tf_op jit(solution)/shard_map/while
  220.2 1.9 copy-start.1
  222.2 5.6 %copy-start.3 = (bf16[8,128,256]{2,1,0:T(8,128)(2,1)}, bf16[8,128,256]{2,1,0:T(8,128)(2,1)S(1)}, u32[]{:S(2)}) copy-start(bf16[8,128,256]{2,1,0:T(8,128)(2,1)S(1)} %get-tuple-element.209) | copy-start | bytes 1572868 | tf_op jit(solution)/shard_map/while
  230.5 1.2 copy-start.2
  233.9 2.3 copy-start
  236.2 3.5 copy-start.6
  236.2 5.4 %copy-start.4 = (bf16[8,128,256]{2,1,0:T(8,128)(2,1)S(1)}, bf16[8,128,256]{2,1,0:T(8,128)(2,1)}, u32[]{:S(2)}) copy-start(bf16[8,128,256]{2,1,0:T(8,128)(2,1)} %copy-done.3) | copy-start | bytes 1572868 | tf_op jit(solution)/shard_map/while
  239.7 1.9 copy-start.1
  241.6 5.6 %copy-start.3 = (bf16[8,128,256]{2,1,0:T(8,128)(2,1)}, bf16[8,128,256]{2,1,0:T(8,128)(2,1)S(1)}, u32[]{:S(2)}) copy-start(bf16[8,128,256]{2,1,0:T(8,128)(2,1)S(1)} %get-tuple-element.209) | copy-start | bytes 1572868 | tf_op jit(solution)/shard_map/while
  249.9 1.2 copy-start.2
  253.3 2.3 copy-start
  255.7 3.5 copy-start.6
  255.7 5.4 %copy-start.4 = (bf16[8,128,256]{2,1,0:T(8,128)(2,1)S(1)}, bf16[8,128,256]{2,1,0:T(8,128)(2,1)}, u32[]{:S(2)}) copy-start(bf16[8,128,256]{2,1,0:T(8,128)(2,1)} %copy-done.3) | copy-start | bytes 1572868 | tf_op jit(solution)/shard_map/while
  259.2 1.9 copy-start.1
  263.7 43.3 %all-to-all-start = ((f32[32,32,256]{2,1,0:T(8,128)}), f32[32,32,256]{2,1,0:T(8,128)S(1)}, u32[]{:S(2)}, u32[]{:S(2)}) async-start(f32[32,32,256]{2,1,0:T(8,128)} %bitcast.6), calls=%async_computation | async-start | bytes 2097152 | tf_op jit(solution)/shard_map/all_to_all | solution.py:23
  307.0 53.8 %all-to-all-start.1 = ((f32[8,512,256]{2,1,0:T(8,128)}), f32[8,512,256]{2,1,0:T(8,128)}, u32[]{:S(2)}, u32[]{:S(2)}) async-start(f32[8,512,256]{2,1,0:T(8,128)} %bitcast.50), calls=%async_computation.1 | async-start | bytes 8388608 | tf_op jit(solution)/shard_map/all_to_all | solution.py:23
  (6 other events, 7.4 us)
Sparse Core Ops, SparseCore 0:
  10.4 106.4 all-gather.1
where the time goes:
time: 371 us
  blocking collectives  96.8 us (26%)
  local copies, waits for them, and re-layouts  89 us (24%)
  waiting for transfers between devices  68.4 us (18%)
  matrix products  56.4 us (15%)
  starting transfers between devices  24.2 us (7%)
  other arithmetic  20.4 us (5%)
  between operations  14.8 us (4%)
    all_to_all x2, waiting for transfers between devices, sent_and_summed(): lax.all_to_all(tiles, axis, split_axis=0, concat_axis=0, tiled=True)  65.4 us
    all_gather x1, blocking collectives, on_device(): lax.all_gather(user_factors, 'ia', axis=0, tiled=True)  51.9 us
    all_gather x1, blocking collectives, on_device(): lax.all_gather(user_tangent, 'ia', axis=0, tiled=True)  44.9 us
    dot_general x7, matrix products, one_turn(): jnp.einsum('gk,gbr->kbr', onehot_cols, to_item, precision=lax.Precision.H...  24.2 us
    all_to_all x2, starting transfers between devices, sent_and_summed(): lax.all_to_all(tiles, axis, split_axis=0, concat_axis=0, tiled=True)  24.2 us
    while x98, local copies, waits for them, and re-layouts  24.1 us
    gather x7, local copies, waits for them, and re-layouts, one_turn(): dvrow = itan_tiles[csel]  22.1 us
    dot_general x7, matrix products, one_turn(): jnp.einsum('gk,gar->kar', onehot_rows, to_user, precision=lax.Precision.H...  16 us
  transfers between devices with their start and end apart: 3, of which 3 were waited for; matrix products, arithmetic and copies ran while one was open for 4% of the time, Pallas kernels for 0%

commit v1 on v0

v1 whole, which is shorter than its diff:
```python
import jax
import jax.numpy as jnp
from jax import lax
from jax.experimental import pallas as pl
from jax.experimental.pallas import tpu as pltpu
from jax.sharding import PartitionSpec as P

MESH = pl.DeviceIdType.MESH
NT = (((1,), (1,)), ((), ()))
TN = (((0,), (0,)), ((), ()))
NN = (((1,), (0,)), ((), ()))
ORDER = (0, 1, 3, 2)
N_SEM = 96


def dot(a, b, dims):
    return lax.dot_general(a, b, dims, preferred_element_type=jnp.float32)


def kernel(
    uf, ut, vf, vt, mask, ou, oi,
    G, Z, mb, Mx, PU, PV, R1, S1, R2, S2, R3, RI1, SI, RI2, send, recv,
):
    au, ia = lax.axis_index("au"), lax.axis_index("ia")
    y, zl = lax.div(au, 2), lax.rem(au, 2)
    zh, x, c = lax.div(ia, 8), lax.rem(lax.div(ia, 2), 4), lax.rem(ia, 2)
    rows = uf.shape[0]
    items, width = vf.shape

    def dev(dx=0, dy=0, dz=0, sib=False, mate=False):
        z = 1 - zl if mate else zl
        core = 1 - c if sib else c
        return (
            lax.rem(y + dy, 4) * 2 + z,
            (lax.rem(zh + dz, 4) * 4 + lax.rem(x + dx, 4)) * 2 + core,
        )

    partners = [dev(sib=True), dev(mate=True)]
    for d in (1, 2, 3):
        partners += [dev(dx=d), dev(dy=d), dev(dz=d)]
    barrier = pltpu.get_barrier_semaphore()
    for p in partners:
        pl.semaphore_signal(barrier, inc=1, device_id=p, device_id_type=MESH)

    G[0, 0, :, :width] = ut[...]
    G[0, 0, :, width:] = uf[...]
    Z[0, :, :width] = vf[...]
    Z[0, :, width:] = vt[...]
    mb[0, 0] = jnp.zeros(mb.shape[2:], jnp.float32)
    mb[0, 0, :, : mask.shape[1]] = mask[...].astype(jnp.float32)

    made = []

    def copy(src, dst, device):
        i = len(made)
        made.append(
            pltpu.make_async_remote_copy(
                src_ref=src,
                dst_ref=dst,
                send_sem=send.at[i],
                recv_sem=recv.at[i],
                device_id=device,
                device_id_type=MESH,
            )
        )
        return made[-1]

    def along(axis, d):
        return dev(dx=d) if axis == 0 else dev(dy=d)

    far = (1, 3, 2)
    by_z = {
        ORDER.index(4 - d): copy(G.at[0, 0], G.at[ORDER.index(4 - d), 0], dev(dz=d))
        for d in far
    }
    first = [
        [copy(G.at[k, 0], G.at[k, 4 - d], along(k % 2, d)) for d in far]
        for k in range(4)
    ]
    second = [
        [
            copy(
                G.at[k, pl.ds(0, 4)],
                G.at[k, pl.ds(4 * (4 - d), 4)],
                along(1 - k % 2, d),
            )
            for d in far
        ]
        for k in range(4)
    ]
    mask_y = [copy(mb.at[0, 0], mb.at[0, 4 - d], dev(dy=d)) for d in far]
    mask_c = copy(mb.at[0], mb.at[1], dev(sib=True))
    item_m = copy(Z.at[0], Z.at[2], dev(mate=True))
    item_s = copy(Z.at[0], Z.at[1], dev(sib=True))
    item_f = copy(Z.at[2], Z.at[3], dev(sib=True))
    back1 = [
        [
            copy(PU.at[k, pl.ds(4 * d, 4)], R1.at[k, d - 1], along(1 - k % 2, d))
            for d in far
        ]
        for k in range(4)
    ]
    back2 = [
        [copy(S1.at[k, d], R2.at[k, d - 1], along(k % 2, d)) for d in far]
        for k in range(4)
    ]
    back3 = [copy(S2.at[k], R3.at[k - 1], dev(dz=ORDER[k])) for k in (1, 2, 3)]
    sum_s0 = copy(PV.at[1], RI1.at[0], dev(sib=True))
    sum_s1 = copy(PV.at[3], RI1.at[1], dev(sib=True))
    sum_m = copy(SI, RI2, dev(mate=True))

    def start(copies):
        for cp in copies:
            cp.start()

    def arrive(copies):
        for cp in copies:
            cp.wait_recv()

    pl.semaphore_wait(barrier, len(partners))
    start(by_z[k] for k in (1, 2, 3))
    start(first[0])
    start(mask_y)
    item_m.start()
    item_s.start()
    PU[...] = jnp.zeros_like(PU)
    PV[...] = jnp.zeros_like(PV)
    for k in (1, 2):
        by_z[k].wait_recv()
        start(first[k])
    arrive(first[0])
    start(second[0])
    arrive(first[1])
    start(second[1])
    by_z[3].wait_recv()
    start(first[3])
    arrive(mask_y)
    mask_c.start()
    arrive(first[2])
    start(second[2])
    arrive(first[3])
    start(second[3])
    mask_c.wait_recv()

    for p in range(2):
        zone = zl if p == 0 else 1 - zl
        j = lax.broadcasted_iota(jnp.int32, (128, items), 0)
        l = lax.broadcasted_iota(jnp.int32, (128, items), 1)
        pick = (j == 4 * (y * 2 + zone) + l // 128).astype(jnp.bfloat16)
        for cc in range(2):
            seen = dot(mb[cc].reshape(32, 128).astype(jnp.bfloat16), pick, NN)
            seen = seen.astype(jnp.bfloat16)
            for k in range(4):
                slot = lax.broadcasted_iota(jnp.int32, (128, 32), 0) // 8
                row = lax.broadcasted_iota(jnp.int32, (128, 32), 1)
                hi, lo = slot // 4, slot % 4
                dy, dx = (hi, lo) if k % 2 == 0 else (lo, hi)
                block = lax.rem(zh + ORDER[k], 4) * 2 + ((x + dx) % 4) // 2
                put = (row == dy * 8 + block).astype(jnp.bfloat16)
                Mx[k, p, :, :, pl.ds(cc * items, items)] = dot(put, seen, NN).reshape(
                    16, 8, items
                )
    item_s.wait_recv()

    def sum1(k):
        arrive(back1[k])
        S1[k] = (PU[k, pl.ds(0, 4)] + R1[k, 0]) + (R1[k, 1] + R1[k, 2])
        start(back2[k])

    def sum2(k):
        arrive(back2[k])
        S2[k] = (S1[k, 0] + R2[k, 0]) + (R2[k, 1] + R2[k, 2])
        if k:
            back3[k - 1].start()

    def step(i, carry):
        p, k = lax.div(i, 4), lax.rem(i, 4)
        for n in range(4):
            @pl.when(i == n)
            def _():
                arrive(second[n])

        @pl.when(i == 4)
        def _():
            item_f.wait_recv()

        w = G[k].reshape(16 * rows, 2 * width)
        z = Z[pl.ds(2 * p, 2)].reshape(2 * items, 2 * width)
        s = dot(w[:, width:], z[:, :width], NT)
        t = dot(w, z, NT)
        e = jnp.exp(jnp.abs(s) * (-1.0 / 16.0))
        r = 1.0 / (1.0 + e)
        cu = (e * r * r * t).reshape(16, 4, 8, 2 * items) * Mx[k, p][:, None]
        cu = cu.reshape(16 * rows, 2 * items).astype(jnp.bfloat16)
        PU[k] += dot(cu, z[:, :width], NN).reshape(16, rows, width)
        PV[pl.ds(2 * p, 2)] += dot(cu, w[:, width:], TN).reshape(2, items, width)

        @pl.when(i == 2)
        def _():
            item_m.wait_recv()
            item_f.start()

        @pl.when(i == 3)
        def _():
            sum_s0.start()

        for n in range(4):
            @pl.when(i == 4 + n)
            def _():
                start(back1[n])

        @pl.when(i == 6)
        def _():
            sum1(0)

        return carry

    lax.fori_loop(0, 8, step, 0)
    sum_s1.start()
    sum1(1)
    sum_s1.wait_recv()
    SI[...] = PV[2] + RI1[1]
    sum_m.start()
    sum2(0)
    sum2(1)
    sum1(2)
    sum1(3)
    sum2(2)
    sum2(3)
    arrive(back3)
    out = 1.0 / 256.0
    ou[...] = ((S2[0] + R3[0]) + (R3[1] + R3[2])) * out
    sum_s0.wait_recv()
    sum_m.wait_recv()
    oi[...] = (PV[0] + RI1[0] + RI2[...]) * out
    for cp in made:
        cp.wait_send()


def on_device(user_factors, item_factors, user_tangent, item_tangent, block_mask):
    rows, width = user_factors.shape
    items = item_factors.shape[0]
    f32, bf16 = jnp.float32, jnp.bfloat16
    vmem = pl.BlockSpec(memory_space=pltpu.VMEM)
    scratch = [
        pltpu.VMEM((4, 16, rows, 2 * width), bf16),
        pltpu.VMEM((4, items, 2 * width), bf16),
        pltpu.VMEM((2, 4, 8, 128), f32),
        pltpu.VMEM((4, 2, 16, 8, 2 * items), f32),
        pltpu.VMEM((4, 16, rows, width), f32),
        pltpu.VMEM((4, items, width), f32),
        pltpu.VMEM((4, 3, 4, rows, width), f32),
        pltpu.VMEM((4, 4, rows, width), f32),
        pltpu.VMEM((4, 3, rows, width), f32),
        pltpu.VMEM((4, rows, width), f32),
        pltpu.VMEM((3, rows, width), f32),
        pltpu.VMEM((2, items, width), f32),
        pltpu.VMEM((items, width), f32),
        pltpu.VMEM((items, width), f32),
        pltpu.SemaphoreType.DMA((N_SEM,)),
        pltpu.SemaphoreType.DMA((N_SEM,)),
    ]
    return pl.pallas_call(
        kernel,
        out_shape=(
            jax.ShapeDtypeStruct((rows, width), f32),
            jax.ShapeDtypeStruct((items, width), f32),
        ),
        in_specs=[vmem] * 5,
        out_specs=[vmem] * 2,
        scratch_shapes=scratch,
        compiler_params=pltpu.CompilerParams(
            collective_id=0, has_side_effects=True, vmem_limit_bytes=56 << 20
        ),
    )(user_factors, user_tangent, item_factors, item_tangent, block_mask)


def solution(mesh):
    placed = (
        P(("au", "ia"), None),
        P(("ia", "au"), None),
        P(("au", "ia"), None),
        P(("ia", "au"), None),
        P("au", "ia"),
    )
    return jax.shard_map(
        on_device,
        mesh=mesh,
        in_specs=placed,
        out_specs=(P(("au", "ia"), None), P(("ia", "au"), None)),
        check_vma=False,
    )
```

time: 371 us -> 72.2 us (0.19)
  blocking collectives: 96.8 us -> 0 us
  local copies, waits for them, and re-layouts: 89 us -> 3.24 us
  waiting for transfers between devices: 68.4 us -> 0 us
  Pallas kernels: 0 us -> 67.9 us
  matrix products: 56.4 us -> 0 us
  starting transfers between devices: 24.2 us -> 0 us
  other arithmetic: 20.4 us -> 0 us
  between operations: 14.8 us -> 0.64 us
    all_gather x2 -> x0, blocking collectives: 96.8 us -> none  [the longest x1 51.9 us: on_device(): lax.all_gather(user_factors, 'ia', axis=0, tiled=True)]
    pallas_call x0 -> x1, Pallas kernels: none -> 67.9 us  [on_device(): pl.pallas_call(kernel, out_shape=(jax.ShapeDtypeStruct((rows, width), f32...]
    all_to_all x2 -> x0, waiting for transfers between devices: 65.4 us -> none  [sent_and_summed(): lax.all_to_all(tiles, axis, split_axis=0, concat_axis=0, tiled=True)]
    dot_general x49 -> x0, matrix products: 56.4 us -> none  [the longest x7 24.2 us: one_turn(): jnp.einsum('gk,gbr->kbr', onehot_cols, to_item, precision=lax.Precision.H...]
    gather x29 -> x0, local copies, waits for them, and re-layouts: 55.5 us -> none  [the longest x7 22.1 us: one_turn(): dvrow = itan_tiles[csel]]
    all_to_all x2 -> x0, starting transfers between devices: 24.2 us -> none  [sent_and_summed(): lax.all_to_all(tiles, axis, split_axis=0, concat_axis=0, tiled=True)]
    while x98 -> x0, local copies, waits for them, and re-layouts: 24.1 us -> none
    mul x2 -> x0, other arithmetic: 9.41 us -> none  [the longest x1 6.86 us: region_pass(): acc_item * scaling]
  transfers between devices with their start and end apart: 3 -> 0, of which waited for: 3 -> 0; matrix products, arithmetic and copies ran while one was open for 4% -> 0% of each run, Pallas kernels for 0% -> 0%
where the time goes in v1:
time: 72.2 us; the launch traced here: 71.8 us
  Pallas kernels  67.9 us (94%)
  local copies, waits for them, and re-layouts  3.24 us (4%)
    pallas_call x1, Pallas kernels, on_device(): pl.pallas_call(kernel, out_shape=(jax.ShapeDtypeStruct((rows, width), f32...  67.9 us
    unnamed x2, local copies, waits for them, and re-layouts  3.24 us

profile of v1, /device:TPU:1, one launch (start us, length us, event | category | flops | bytes accessed | tf_op | source)
XLA Modules:
  0.0 71.8 jit_solution(12655053794899408390)
XLA Ops:
  0.6 67.9 %shard_map.68 = (f32[32,256]{1,0:T(8,128)}, f32[512,256]{1,0:T(8,128)}) custom-call(bf16[32,256]{1,0:T(8,128)(2,1)} %uf.1, bf16[32,256]{1,0:T(8,128)(2,1)} %ut.1, bf16[512,256]{1,0:T(8,128)(2,1)} %vf.1, bf16[512,256]{1,0:T(8,128)(2,1)} %vt.1, s32[8,32]{1,0:T(8,128)} %mask.1), custom_call_target="tpu_custom_call" | custom-call | tf_op jit(solution)/shard_map/pallas_call | solution.py:263
  68.5 1.4 %copy.9 = f32[32,256]{1,0:T(8,128)} copy(f32[32,256]{1,0:T(8,128)} %get-tuple-element.4) | data formatting | bytes 65536
  69.9 1.9 %copy.10 = f32[512,256]{1,0:T(8,128)} copy(f32[512,256]{1,0:T(8,128)} %get-tuple-element.5) | data formatting | bytes 1048576

commit v2 on v1

v2 whole, which is shorter than its diff:
```python
import jax
import jax.numpy as jnp
from jax import lax
from jax.experimental import pallas as pl
from jax.experimental.pallas import tpu as pltpu
from jax.sharding import PartitionSpec as P

MESH = pl.DeviceIdType.MESH
NT = (((1,), (1,)), ((), ()))
TN = (((0,), (0,)), ((), ()))
NN = (((1,), (0,)), ((), ()))
ORDER = (0, 1, 3, 2)
N_SEM = 112


def dot(a, b, dims):
    return lax.dot_general(a, b, dims, preferred_element_type=jnp.float32)


def kernel(
    uf, ut, vf, vt, mask, ou, oi,
    G, Z, mi, mb, Mx, PU, PV, R1, S1, R2, S2, R3, RI1, SI, RI2, send, recv, local,
):
    au, ia = lax.axis_index("au"), lax.axis_index("ia")
    y, zl = lax.div(au, 2), lax.rem(au, 2)
    zh, x, c = lax.div(ia, 8), lax.rem(lax.div(ia, 2), 4), lax.rem(ia, 2)
    rows, width = uf.shape
    items = vf.shape[0]
    half = rows // 2

    def dev(dx=0, dy=0, dz=0, sib=False, mate=False):
        z = 1 - zl if mate else zl
        core = 1 - c if sib else c
        return (
            lax.rem(y + dy, 4) * 2 + z,
            (lax.rem(zh + dz, 4) * 4 + lax.rem(x + dx, 4)) * 2 + core,
        )

    partners = [dev(sib=True), dev(mate=True)]
    for d in (1, 2, 3):
        partners += [dev(dx=d), dev(dy=d), dev(dz=d)]
    barrier = pltpu.get_barrier_semaphore()
    for p in partners:
        pl.semaphore_signal(barrier, inc=1, device_id=p, device_id_type=MESH)

    left, right = pl.ds(0, width), pl.ds(width, width)
    place = [
        pltpu.make_async_copy(ut, G.at[0, 0, 0, :, left], local.at[0]),
        pltpu.make_async_copy(uf, G.at[0, 0, 0, :, right], local.at[1]),
        pltpu.make_async_copy(mask, mi, local.at[2]),
        pltpu.make_async_copy(vf, Z.at[0, :, left], local.at[3]),
        pltpu.make_async_copy(vt, Z.at[0, :, right], local.at[4]),
    ]
    for cp in place:
        cp.start()

    made = []

    def copy(src, dst, device):
        i = len(made)
        made.append(
            pltpu.make_async_remote_copy(
                src_ref=src,
                dst_ref=dst,
                send_sem=send.at[i],
                recv_sem=recv.at[i],
                device_id=device,
                device_id_type=MESH,
            )
        )
        return made[-1]

    far = (1, 3, 2)
    h0, h1 = pl.ds(0, half), pl.ds(half, half)
    al = pl.ds(0, 4)
    by_z = {
        ORDER.index(4 - d): copy(
            G.at[0, 0, 0], G.at[ORDER.index(4 - d), 0, 0], dev(dz=d)
        )
        for d in far
    }
    first, second = [], []
    for k in range(4):
        first.append((
            [copy(G.at[k, 0, 0, h0], G.at[k, 0, 4 - d, h0], dev(dx=d)) for d in far],
            [copy(G.at[k, 0, 0, h1], G.at[k, 4 - d, 0, h1], dev(dy=d)) for d in far],
        ))
        second.append((
            [copy(G.at[k, 0, al, h0], G.at[k, 4 - d, al, h0], dev(dy=d)) for d in far],
            [copy(G.at[k, al, 0, h1], G.at[k, al, 4 - d, h1], dev(dx=d)) for d in far],
        ))
    mask_y = [copy(mb.at[0, 0], mb.at[0, 4 - d], dev(dy=d)) for d in far]
    mask_c = copy(mb.at[0], mb.at[1], dev(sib=True))
    item_m = copy(Z.at[0], Z.at[2], dev(mate=True))
    item_s = copy(Z.at[0], Z.at[1], dev(sib=True))
    item_f = copy(Z.at[2], Z.at[3], dev(sib=True))
    back1, back2 = [], []
    for k in range(4):
        back1.append((
            [copy(PU.at[k, d, al, h0], R1.at[k, d - 1, 0], dev(dy=d)) for d in far],
            [copy(PU.at[k, al, d, h1], R1.at[k, d - 1, 1], dev(dx=d)) for d in far],
        ))
        back2.append((
            [copy(S1.at[k, 0, d], R2.at[k, d - 1, 0], dev(dx=d)) for d in far],
            [copy(S1.at[k, 1, d], R2.at[k, d - 1, 1], dev(dy=d)) for d in far],
        ))
    back3 = [copy(S2.at[k], R3.at[k - 1], dev(dz=ORDER[k])) for k in (1, 2, 3)]
    sum_s0 = copy(PV.at[1], RI1.at[0], dev(sib=True))
    sum_s1 = copy(PV.at[3], RI1.at[1], dev(sib=True))
    sum_m = copy(SI, RI2, dev(mate=True))

    def start(copies):
        for cp in copies:
            cp.start()

    def arrive(copies):
        for cp in copies:
            cp.wait_recv()

    def begin(pair):
        start(pair[0])
        start(pair[1])

    def after(came, then):
        for n in range(2):
            arrive(came[n])
            start(then[n])

    place[0].wait()
    place[1].wait()
    pl.semaphore_wait(barrier, len(partners))
    start(by_z[k] for k in (1, 2, 3))
    begin(first[0])
    place[3].wait()
    place[4].wait()
    item_m.start()
    item_s.start()
    place[2].wait()
    mb[0, 0] = jnp.zeros(mb.shape[2:], jnp.float32)
    mb[0, 0, :, : mask.shape[1]] = mi[...].astype(jnp.float32)
    start(mask_y)
    PU[...] = jnp.zeros_like(PU)
    PV[...] = jnp.zeros_like(PV)
    by_z[1].wait_recv()
    begin(first[1])
    by_z[2].wait_recv()
    begin(first[2])
    after(first[0], second[0])
    by_z[3].wait_recv()
    begin(first[3])
    arrive(mask_y)
    mask_c.start()
    after(first[1], second[1])
    after(first[2], second[2])
    after(first[3], second[3])
    mask_c.wait_recv()

    for p in range(2):
        zone = zl if p == 0 else 1 - zl
        j = lax.broadcasted_iota(jnp.int32, (128, items), 0)
        l = lax.broadcasted_iota(jnp.int32, (128, items), 1)
        pick = (j == 4 * (y * 2 + zone) + l // 128).astype(jnp.bfloat16)
        for cc in range(2):
            seen = dot(mb[cc].reshape(32, 128).astype(jnp.bfloat16), pick, NN)
            seen = seen.astype(jnp.bfloat16)
            for k in range(4):
                slot = lax.broadcasted_iota(jnp.int32, (128, 32), 0) // 8
                row = lax.broadcasted_iota(jnp.int32, (128, 32), 1)
                dy, dx = slot // 4, slot % 4
                block = lax.rem(zh + ORDER[k], 4) * 2 + ((x + dx) % 4) // 2
                put = (row == dy * 8 + block).astype(jnp.bfloat16)
                Mx[k, p, :, :, pl.ds(cc * items, items)] = dot(put, seen, NN).reshape(
                    16, 8, items
                )
    item_s.wait_recv()

    def sum1(k):
        own = (PU[k, 0, :, h0], PU[k, :, 0, h1])
        for n in range(2):
            arrive(back1[k][n])
            S1[k, n] = (own[n] + R1[k, 0, n]) + (R1[k, 1, n] + R1[k, 2, n])
            start(back2[k][n])

    def sum2(k):
        for n, h in ((0, h0), (1, h1)):
            arrive(back2[k][n])
            S2[k, h] = (S1[k, n, 0] + R2[k, 0, n]) + (R2[k, 1, n] + R2[k, 2, n])
        if k:
            back3[k - 1].start()

    tile = items // 2

    def step(i, carry):
        p = lax.div(i, 4)
        k = lax.rem(i + p, 4)
        for n in range(4):
            @pl.when(i == n)
            def _():
                arrive(second[n][0])
                arrive(second[n][1])

        @pl.when(i == 4)
        def _():
            item_f.wait_recv()

        w = G[k].reshape(16 * rows, 2 * width)

        def front(q):
            z = Z[2 * p + q // 2, pl.ds((q % 2) * tile, tile)]
            return z, dot(w[:, width:], z[:, :width], NT), dot(w, z, NT)

        def rear(q, z, s, t):
            e = jnp.exp(jnp.abs(s) * (-1.0 / 16.0))
            r = 1.0 / (1.0 + e)
            seen = Mx[k, p, :, :, pl.ds(q * tile, tile)]
            cu = (e * r * r * t).reshape(16, rows // 8, 8, tile) * seen[:, None]
            cu = cu.reshape(16 * rows, tile).astype(jnp.bfloat16)
            PV[2 * p + q // 2, pl.ds((q % 2) * tile, tile)] += dot(cu, w[:, width:], TN)
            return dot(cu, z[:, :width], NN)

        total, held = None, front(0)
        for q in range(4):
            now = held
            if q < 3:
                held = front(q + 1)
            part = rear(q, *now)
            total = part if total is None else total + part
        PU[k] += total.reshape(4, 4, rows, width)

        @pl.when(i == 2)
        def _():
            item_m.wait_recv()
            item_f.start()

        @pl.when(i == 3)
        def _():
            sum_s0.start()

        for n in range(4):
            @pl.when(i == 4 + n)
            def _():
                if n == 3:
                    sum_s1.start()
                begin(back1[(n + 1) % 4])

        return carry

    lax.fori_loop(0, 8, step, 0)
    sum_s1.wait_recv()
    SI[...] = PV[2] + RI1[1]
    sum_m.start()
    sum1(1)
    sum1(2)
    sum2(1)
    sum1(3)
    sum2(2)
    sum1(0)
    sum2(3)
    sum2(0)
    arrive(back3)
    out = 1.0 / 256.0
    ou[...] = ((S2[0] + R3[0]) + (R3[1] + R3[2])) * out
    sum_s0.wait_recv()
    sum_m.wait_recv()
    oi[...] = (PV[0] + RI1[0] + RI2[...]) * out
    for cp in made:
        cp.wait_send()


def on_device(user_factors, item_factors, user_tangent, item_tangent, block_mask):
    rows, width = user_factors.shape
    items = item_factors.shape[0]
    f32, bf16 = jnp.float32, jnp.bfloat16
    vmem = pl.BlockSpec(memory_space=pltpu.VMEM)
    scratch = [
        pltpu.VMEM((4, 4, 4, rows, 2 * width), bf16),
        pltpu.VMEM((4, items, 2 * width), bf16),
        pltpu.VMEM(block_mask.shape, jnp.int32),
        pltpu.VMEM((2, 4, 8, 128), f32),
        pltpu.VMEM((4, 2, 16, 8, 2 * items), f32),
        pltpu.VMEM((4, 4, 4, rows, width), f32),
        pltpu.VMEM((4, items, width), f32),
        pltpu.VMEM((4, 3, 2, 4, rows // 2, width), f32),
        pltpu.VMEM((4, 2, 4, rows // 2, width), f32),
        pltpu.VMEM((4, 3, 2, rows // 2, width), f32),
        pltpu.VMEM((4, rows, width), f32),
        pltpu.VMEM((3, rows, width), f32),
        pltpu.VMEM((2, items, width), f32),
        pltpu.VMEM((items, width), f32),
        pltpu.VMEM((items, width), f32),
        pltpu.SemaphoreType.DMA((N_SEM,)),
        pltpu.SemaphoreType.DMA((N_SEM,)),
        pltpu.SemaphoreType.DMA((5,)),
    ]
    return pl.pallas_call(
        kernel,
        out_shape=(
            jax.ShapeDtypeStruct((rows, width), f32),
            jax.ShapeDtypeStruct((items, width), f32),
        ),
        in_specs=[pl.BlockSpec(memory_space=pl.ANY)] * 5,
        out_specs=[vmem] * 2,
        scratch_shapes=scratch,
        compiler_params=pltpu.CompilerParams(
            collective_id=0, has_side_effects=True, vmem_limit_bytes=40 << 20
        ),
    )(user_factors, user_tangent, item_factors, item_tangent, block_mask)


def solution(mesh):
    placed = (
        P(("au", "ia"), None),
        P(("ia", "au"), None),
        P(("au", "ia"), None),
        P(("ia", "au"), None),
        P("au", "ia"),
    )
    return jax.shard_map(
        on_device,
        mesh=mesh,
        in_specs=placed,
        out_specs=(P(("au", "ia"), None), P(("ia", "au"), None)),
        check_vma=False,
    )
```

time: 72.2 us -> 66.7 us (0.924)
  Pallas kernels: 67.9 us -> 60.3 us
  local copies, waits for them, and re-layouts: 3.24 us -> 5.42 us
    pallas_call x1, Pallas kernels: 67.9 us -> 60.3 us  [on_device(): pl.pallas_call(kernel, out_shape=(jax.ShapeDtypeStruct((rows, width), f32...]
    unnamed x2 -> x12, local copies, waits for them, and re-layouts: 3.24 us -> 5.42 us
where the time goes in v2:
time: 66.7 us; the launch traced here: 66.4 us
  Pallas kernels  60.3 us (90%)
  local copies, waits for them, and re-layouts  5.42 us (8%)
    pallas_call x1, Pallas kernels, on_device(): pl.pallas_call(kernel, out_shape=(jax.ShapeDtypeStruct((rows, width), f32...  60.3 us
    unnamed x12, local copies, waits for them, and re-layouts  5.42 us

profile of v2, /device:TPU:1, one launch (start us, length us, event | category | flops | bytes accessed | tf_op | source)
XLA Modules:
  0.0 66.4 jit_solution(1772086748956721038)
XLA Ops:
  0.6 0.0 copy-start
  0.6 0.9 %copy-done = bf16[512,256]{1,0:T(8,128)(2,1)S(1)} copy-done((bf16[512,256]{1,0:T(8,128)(2,1)S(1)}, bf16[512,256]{1,0:T(8,128)(2,1)}, u32[]{:S(2)}) %copy-start) | copy-done | bytes 262168
  1.6 0.0 copy-start.1
  1.6 0.9 %copy-done.1 = bf16[512,256]{1,0:T(8,128)(2,1)S(1)} copy-done((bf16[512,256]{1,0:T(8,128)(2,1)S(1)}, bf16[512,256]{1,0:T(8,128)(2,1)}, u32[]{:S(2)}) %copy-start.1) | copy-done | bytes 262168
  2.5 0.0 copy-start.2
  2.5 0.7 %copy-done.2 = bf16[32,256]{1,0:T(8,128)(2,1)S(1)} copy-done((bf16[32,256]{1,0:T(8,128)(2,1)S(1)}, bf16[32,256]{1,0:T(8,128)(2,1)}, u32[]{:S(2)}) %copy-start.2) | copy-done | bytes 16408
  3.3 0.0 copy-start.3
  3.3 0.7 %copy-done.3 = bf16[32,256]{1,0:T(8,128)(2,1)S(1)} copy-done((bf16[32,256]{1,0:T(8,128)(2,1)S(1)}, bf16[32,256]{1,0:T(8,128)(2,1)}, u32[]{:S(2)}) %copy-start.3) | copy-done | bytes 16408
  4.0 0.0 copy-start.4
  4.0 0.7 %copy-done.4 = s32[8,32]{1,0:T(8,128)S(1)} copy-done((s32[8,32]{1,0:T(8,128)S(1)}, s32[8,32]{1,0:T(8,128)}, u32[]{:S(2)}) %copy-start.4) | copy-done | bytes 1048
  4.7 60.3 %shard_map.68 = (f32[32,256]{1,0:T(8,128)S(1)}, f32[512,256]{1,0:T(8,128)S(1)}) custom-call(bf16[32,256]{1,0:T(8,128)(2,1)S(1)} %copy-done.2, bf16[32,256]{1,0:T(8,128)(2,1)S(1)} %copy-done.3, bf16[512,256]{1,0:T(8,128)(2,1)S(1)} %copy-done, bf16[512,256]{1,0:T(8,128)(2,1)S(1)} %copy-done.1, s32[8,32]{1,0:T(8,128)S(1)} %copy-done.4), custom_call_target="tpu_custom_call" | custom-call | tf_op jit(solution)/shard_map/pallas_call | solution.py:295
  65.0 0.6 copy.9
  65.6 0.8 %copy.10 = f32[512,256]{1,0:T(8,128)} copy(f32[512,256]{1,0:T(8,128)S(1)} %get-tuple-element.5) | data formatting | bytes 1048576
Async XLA Ops:
  0.6 1.0 %copy-start = (bf16[512,256]{1,0:T(8,128)(2,1)S(1)}, bf16[512,256]{1,0:T(8,128)(2,1)}, u32[]{:S(2)}) copy-start(bf16[512,256]{1,0:T(8,128)(2,1)} %vf.1) | copy-start | bytes 786436
  1.6 0.9 %copy-start.1 = (bf16[512,256]{1,0:T(8,128)(2,1)S(1)}, bf16[512,256]{1,0:T(8,128)(2,1)}, u32[]{:S(2)}) copy-start(bf16[512,256]{1,0:T(8,128)(2,1)} %vt.1) | copy-start | bytes 786436
  2.5 0.7 %copy-start.2 = (bf16[32,256]{1,0:T(8,128)(2,1)S(1)}, bf16[32,256]{1,0:T(8,128)(2,1)}, u32[]{:S(2)}) copy-start(bf16[32,256]{1,0:T(8,128)(2,1)} %uf.1) | copy-start | bytes 49156
  3.3 0.7 %copy-start.3 = (bf16[32,256]{1,0:T(8,128)(2,1)S(1)}, bf16[32,256]{1,0:T(8,128)(2,1)}, u32[]{:S(2)}) copy-start(bf16[32,256]{1,0:T(8,128)(2,1)} %ut.1) | copy-start | bytes 49156
  4.0 0.7 %copy-start.4 = (s32[8,32]{1,0:T(8,128)S(1)}, s32[8,32]{1,0:T(8,128)}, u32[]{:S(2)}) copy-start(s32[8,32]{1,0:T(8,128)} %mask.1) | copy-start | bytes 3076

commit v3 on v2

--- a/solution.py
+++ b/solution.py
@@ -10,7 +10,7 @@
 TN = (((0,), (0,)), ((), ()))
 NN = (((1,), (0,)), ((), ()))
 ORDER = (0, 1, 3, 2)
-N_SEM = 112
+N_SEM = 144
 
 
 def dot(a, b, dims):
@@ -19,7 +19,7 @@
 
 def kernel(
     uf, ut, vf, vt, mask, ou, oi,
-    G, Z, mi, mb, Mx, PU, PV, R1, S1, R2, S2, R3, RI1, SI, RI2, send, recv, local,
+    G, Z, mi, mb, Mx, PU, PV, Q1, F1, R1, E1, S1, R2, S2, R3, RI1, QI, FI, R4, E4, send, recv, local,
 ):
     au, ia = lax.axis_index("au"), lax.axis_index("ia")
     y, zl = lax.div(au, 2), lax.rem(au, 2)
@@ -96,10 +96,14 @@
     item_f = copy(Z.at[2], Z.at[3], dev(sib=True))
     back1, back2 = [], []
     for k in range(4):
-        back1.append((
-            [copy(PU.at[k, d, al, h0], R1.at[k, d - 1, 0], dev(dy=d)) for d in far],
-            [copy(PU.at[k, al, d, h1], R1.at[k, d - 1, 1], dev(dx=d)) for d in far],
-        ))
+        pairs = []
+        for n in range(2):
+            pairs.append([])
+            for d in far:
+                to, at = (dev(dx=d) if n else dev(dy=d)), (k, n, d - 1)
+                pairs[n].append(copy(F1.at[at], E1.at[at], to))
+                pairs[n].append(copy(Q1.at[at], R1.at[at], to))
+        back1.append(pairs)
         back2.append((
             [copy(S1.at[k, 0, d], R2.at[k, d - 1, 0], dev(dx=d)) for d in far],
             [copy(S1.at[k, 1, d], R2.at[k, d - 1, 1], dev(dy=d)) for d in far],
@@ -107,7 +111,7 @@
     back3 = [copy(S2.at[k], R3.at[k - 1], dev(dz=ORDER[k])) for k in (1, 2, 3)]
     sum_s0 = copy(PV.at[1], RI1.at[0], dev(sib=True))
     sum_s1 = copy(PV.at[3], RI1.at[1], dev(sib=True))
-    sum_m = copy(SI, RI2, dev(mate=True))
+    sum_m = [copy(FI, E4, dev(mate=True)), copy(QI, R4, dev(mate=True))]
 
     def start(copies):
         for cp in copies:
@@ -174,11 +178,40 @@
                 )
     item_s.wait_recv()
 
+    lanes = (slice(0, 128), slice(128, 256))
+
+    def code(v, q_ref, f_ref):
+        shape = v.shape
+        v = v.reshape(-1, 8, 2 * 128)
+        big = jnp.max(jnp.abs(v), axis=0)
+        big = jnp.maximum(jnp.maximum(big[:, :128], big[:, 128:]), 1e-30)
+        f_ref[...] = big * (1.0 / 32767.0)
+        up = 32767.0 / big
+        for l in lanes:
+            q = jnp.round(v[:, :, l] * up).astype(jnp.int32).astype(jnp.int16)
+            q_ref[..., l] = q.reshape(*shape[:-1], 128)
+
+    def plain(q_ref, f_ref, l):
+        q = q_ref[..., l].astype(jnp.int32).astype(jnp.float32)
+        return (q.reshape(-1, 8, 128) * f_ref[...]).reshape(q.shape)
+
+    def out1(k):
+        for n in range(2):
+            for d in far:
+                v = PU[k, :, d, h1] if n else PU[k, d, :, h0]
+                at = (k, n, d - 1)
+                code(v, Q1.at[at], F1.at[at])
+            start(back1[k][n])
+
     def sum1(k):
-        own = (PU[k, 0, :, h0], PU[k, :, 0, h1])
         for n in range(2):
             arrive(back1[k][n])
-            S1[k, n] = (own[n] + R1[k, 0, n]) + (R1[k, 1, n] + R1[k, 2, n])
+            own = PU[k, :, 0, h1] if n else PU[k, 0, :, h0]
+            for l in lanes:
+                v = own[..., l]
+                for d in (1, 2, 3):
+                    v += plain(R1.at[k, n, d - 1], E1.at[k, n, d - 1], l)
+                S1[k, n, :, :, l] = v
             start(back2[k][n])
 
     def sum2(k):
@@ -241,14 +274,14 @@
             def _():
                 if n == 3:
                     sum_s1.start()
-                begin(back1[(n + 1) % 4])
+                out1((n + 1) % 4)
 
         return carry
 
     lax.fori_loop(0, 8, step, 0)
     sum_s1.wait_recv()
-    SI[...] = PV[2] + RI1[1]
-    sum_m.start()
+    code(PV[2] + RI1[1], QI, FI)
+    start(sum_m)
     sum1(1)
     sum1(2)
     sum2(1)
@@ -261,8 +294,9 @@
     out = 1.0 / 256.0
     ou[...] = ((S2[0] + R3[0]) + (R3[1] + R3[2])) * out
     sum_s0.wait_recv()
-    sum_m.wait_recv()
-    oi[...] = (PV[0] + RI1[0] + RI2[...]) * out
+    arrive(sum_m)
+    for l in lanes:
+        oi[:, l] = (PV[0, :, l] + RI1[0, :, l] + plain(R4, E4, l)) * out
     for cp in made:
         cp.wait_send()
 
@@ -280,31 +314,38 @@
         pltpu.VMEM((4, 2, 16, 8, 2 * items), f32),
         pltpu.VMEM((4, 4, 4, rows, width), f32),
         pltpu.VMEM((4, items, width), f32),
-        pltpu.VMEM((4, 3, 2, 4, rows // 2, width), f32),
+        pltpu.VMEM((4, 2, 3, 4, rows // 2, width), jnp.int16),
+        pltpu.VMEM((4, 2, 3, 8, 128), f32),
+        pltpu.VMEM((4, 2, 3, 4, rows // 2, width), jnp.int16),
+        pltpu.VMEM((4, 2, 3, 8, 128), f32),
         pltpu.VMEM((4, 2, 4, rows // 2, width), f32),
         pltpu.VMEM((4, 3, 2, rows // 2, width), f32),
         pltpu.VMEM((4, rows, width), f32),
         pltpu.VMEM((3, rows, width), f32),
         pltpu.VMEM((2, items, width), f32),
-        pltpu.VMEM((items, width), f32),
-        pltpu.VMEM((items, width), f32),
+        pltpu.VMEM((items, width), jnp.int16),
+        pltpu.VMEM((8, 128), f32),
+        pltpu.VMEM((items, width), jnp.int16),
+        pltpu.VMEM((8, 128), f32),
         pltpu.SemaphoreType.DMA((N_SEM,)),
         pltpu.SemaphoreType.DMA((N_SEM,)),
         pltpu.SemaphoreType.DMA((5,)),
     ]
+    args = (user_factors, user_tangent, item_factors, item_tangent, block_mask)
+    hbm = [pltpu.with_memory_space_constraint(a, pltpu.HBM) for a in args]
     return pl.pallas_call(
         kernel,
         out_shape=(
             jax.ShapeDtypeStruct((rows, width), f32),
             jax.ShapeDtypeStruct((items, width), f32),
         ),
-        in_specs=[pl.BlockSpec(memory_space=pl.ANY)] * 5,
+        in_specs=[pl.BlockSpec(memory_space=pltpu.HBM)] * 5,
         out_specs=[vmem] * 2,
         scratch_shapes=scratch,
         compiler_params=pltpu.CompilerParams(
             collective_id=0, has_side_effects=True, vmem_limit_bytes=40 << 20
         ),
-    )(user_factors, user_tangent, item_factors, item_tangent, block_mask)
+    )(*hbm)
 
 
 def solution(mesh):

time: 66.7 us -> 57.2 us (0.86)
  Pallas kernels: 60.3 us -> 54.7 us
  local copies, waits for them, and re-layouts: 5.42 us -> 1.41 us
    pallas_call x1, Pallas kernels: 60.3 us -> 54.7 us  [on_device(): pl.pallas_call(kernel, out_shape=(jax.ShapeDtypeStruct((rows, width), f32...]
    unnamed x12 -> x2, local copies, waits for them, and re-layouts: 5.42 us -> 1.41 us
where the time goes in v3:
time: 57.2 us; the launch traced here: 56.7 us
  Pallas kernels  54.7 us (96%)
  local copies, waits for them, and re-layouts  1.41 us (2%)
  between operations  0.64 us (1%)
    pallas_call x1, Pallas kernels, on_device(): pl.pallas_call(kernel, out_shape=(jax.ShapeDtypeStruct((rows, width), f32...  54.7 us
    unnamed x2, local copies, waits for them, and re-layouts  1.41 us

profile of v3, /device:TPU:1, one launch (start us, length us, event | category | flops | bytes accessed | tf_op | source)
XLA Modules:
  0.0 56.7 jit_solution(4803401884827306232)
XLA Ops:
  0.6 54.7 %shard_map.68 = (f32[32,256]{1,0:T(8,128)S(1)}, f32[512,256]{1,0:T(8,128)S(1)}) custom-call(bf16[32,256]{1,0:T(8,128)(2,1)} %uf.1, bf16[32,256]{1,0:T(8,128)(2,1)} %ut.1, bf16[512,256]{1,0:T(8,128)(2,1)} %vf.1, bf16[512,256]{1,0:T(8,128)(2,1)} %vt.1, s32[8,32]{1,0:T(8,128)} %mask.1), custom_call_target="tpu_custom_call" | custom-call | tf_op jit(solution)/shard_map/pallas_call | solution.py:336
  55.3 0.6 %copy.9 = f32[32,256]{1,0:T(8,128)} copy(f32[32,256]{1,0:T(8,128)S(1)} %get-tuple-element.4) | data formatting | bytes 65536
  55.9 0.8 %copy.10 = f32[512,256]{1,0:T(8,128)} copy(f32[512,256]{1,0:T(8,128)S(1)} %get-tuple-element.5) | data formatting | bytes 1048576

commit v4 on v3

--- a/solution.py
+++ b/solution.py
@@ -9,8 +9,8 @@
 NT = (((1,), (1,)), ((), ()))
 TN = (((0,), (0,)), ((), ()))
 NN = (((1,), (0,)), ((), ()))
-ORDER = (0, 1, 3, 2)
-N_SEM = 144
+ORDER = (0, 1, 2, 3)
+N_SEM = 56
 
 
 def dot(a, b, dims):
@@ -19,7 +19,7 @@
 
 def kernel(
     uf, ut, vf, vt, mask, ou, oi,
-    G, Z, mi, mb, Mx, PU, PV, Q1, F1, R1, E1, S1, R2, S2, R3, RI1, QI, FI, R4, E4, send, recv, local,
+    G, Z, mi, mb, Mx, PU, PV, Q1, F1, R1, E1, S1, R2, S2, R3, RI1, QI, FI, R4, E4, OU, OI, send, recv, local,
 ):
     au, ia = lax.axis_index("au"), lax.axis_index("ia")
     y, zl = lax.div(au, 2), lax.rem(au, 2)
@@ -56,84 +56,119 @@
 
     made = []
 
+    class Set:
+        def __init__(self, land, copies):
+            n = len(made)
+            made.append(self)
+
+            def describe(src, dst, device):
+                return pltpu.make_async_remote_copy(
+                    src_ref=src,
+                    dst_ref=dst,
+                    send_sem=send.at[n],
+                    recv_sem=recv.at[n],
+                    device_id=device,
+                    device_id_type=MESH,
+                )
+
+            self.copies = [describe(*cp) for cp in copies]
+            self.all = describe(land, land, copies[0][2])
+
+        def start(self):
+            for cp in self.copies:
+                cp.start()
+
+        def wait_recv(self):
+            self.all.wait_recv()
+
+        def wait_send(self):
+            self.all.wait_send()
+
     def copy(src, dst, device):
-        i = len(made)
-        made.append(
-            pltpu.make_async_remote_copy(
-                src_ref=src,
-                dst_ref=dst,
-                send_sem=send.at[i],
-                recv_sem=recv.at[i],
-                device_id=device,
-                device_id_type=MESH,
-            )
-        )
-        return made[-1]
+        return Set(dst, [(src, dst, device)])
 
     far = (1, 3, 2)
     h0, h1 = pl.ds(0, half), pl.ds(half, half)
-    al = pl.ds(0, 4)
-    by_z = {
-        ORDER.index(4 - d): copy(
-            G.at[0, 0, 0], G.at[ORDER.index(4 - d), 0, 0], dev(dz=d)
-        )
-        for d in far
-    }
+    al, rest = pl.ds(0, 4), pl.ds(1, 3)
+    by_z = {}
+    for d in far:
+        k = ORDER.index(4 - d)
+        by_z[k] = copy(G.at[0, 0, 0], G.at[k, 0, 0], dev(dz=d))
     first, second = [], []
     for k in range(4):
+        own = (G.at[k, 0, 0, h0], G.at[k, 0, 0, h1])
         first.append((
-            [copy(G.at[k, 0, 0, h0], G.at[k, 0, 4 - d, h0], dev(dx=d)) for d in far],
-            [copy(G.at[k, 0, 0, h1], G.at[k, 4 - d, 0, h1], dev(dy=d)) for d in far],
+            Set(
+                G.at[k, 0, rest, h0],
+                [(own[0], G.at[k, 0, 4 - d, h0], dev(dx=d)) for d in far],
+            ),
+            Set(
+                G.at[k, rest, 0, h1],
+                [(own[1], G.at[k, 4 - d, 0, h1], dev(dy=d)) for d in far],
+            ),
         ))
+        own = (G.at[k, 0, al, h0], G.at[k, al, 0, h1])
         second.append((
-            [copy(G.at[k, 0, al, h0], G.at[k, 4 - d, al, h0], dev(dy=d)) for d in far],
-            [copy(G.at[k, al, 0, h1], G.at[k, al, 4 - d, h1], dev(dx=d)) for d in far],
+            Set(
+                G.at[k, rest, al, h0],
+                [(own[0], G.at[k, 4 - d, al, h0], dev(dy=d)) for d in far],
+            ),
+            Set(
+                G.at[k, al, rest, h1],
+                [(own[1], G.at[k, al, 4 - d, h1], dev(dx=d)) for d in far],
+            ),
         ))
-    mask_y = [copy(mb.at[0, 0], mb.at[0, 4 - d], dev(dy=d)) for d in far]
+    mask_y = Set(
+        mb.at[0, rest], [(mb.at[0, 0], mb.at[0, 4 - d], dev(dy=d)) for d in far]
+    )
     mask_c = copy(mb.at[0], mb.at[1], dev(sib=True))
     item_m = copy(Z.at[0], Z.at[2], dev(mate=True))
     item_s = copy(Z.at[0], Z.at[1], dev(sib=True))
     item_f = copy(Z.at[2], Z.at[3], dev(sib=True))
+    gathers = list(made)
     back1, back2 = [], []
     for k in range(4):
-        pairs = []
+        scales, sums, onward = [], [], []
         for n in range(2):
-            pairs.append([])
-            for d in far:
-                to, at = (dev(dx=d) if n else dev(dy=d)), (k, n, d - 1)
-                pairs[n].append(copy(F1.at[at], E1.at[at], to))
-                pairs[n].append(copy(Q1.at[at], R1.at[at], to))
-        back1.append(pairs)
-        back2.append((
-            [copy(S1.at[k, 0, d], R2.at[k, d - 1, 0], dev(dx=d)) for d in far],
-            [copy(S1.at[k, 1, d], R2.at[k, d - 1, 1], dev(dy=d)) for d in far],
-        ))
-    back3 = [copy(S2.at[k], R3.at[k - 1], dev(dz=ORDER[k])) for k in (1, 2, 3)]
+            to = [(d, dev(dx=d) if n else dev(dy=d)) for d in far]
+            scales.append(
+                Set(E1.at[k, n], [(F1.at[k, n, d - 1], E1.at[k, n, d - 1], t) for d, t in to])
+            )
+            sums.append(
+                Set(R1.at[k, n], [(Q1.at[k, n, d - 1], R1.at[k, n, d - 1], t) for d, t in to])
+            )
+            to = [(d, dev(dy=d) if n else dev(dx=d)) for d in far]
+            onward.append(
+                Set(R2.at[k, n], [(S1.at[k, n, d], R2.at[k, n, d - 1], t) for d, t in to])
+            )
+        back1.append((scales, sums))
+        back2.append(onward)
+    back3 = Set(R3, [(S2.at[k], R3.at[k - 1], dev(dz=ORDER[k])) for k in (1, 2, 3)])
     sum_s0 = copy(PV.at[1], RI1.at[0], dev(sib=True))
     sum_s1 = copy(PV.at[3], RI1.at[1], dev(sib=True))
-    sum_m = [copy(FI, E4, dev(mate=True)), copy(QI, R4, dev(mate=True))]
-
-    def start(copies):
-        for cp in copies:
-            cp.start()
-
-    def arrive(copies):
-        for cp in copies:
-            cp.wait_recv()
-
-    def begin(pair):
-        start(pair[0])
-        start(pair[1])
+    quarter = items // 4
+    sum_m = [copy(FI, E4, dev(mate=True))]
+    for n in range(4):
+        part = pl.ds(n * quarter, quarter)
+        sum_m.append(copy(QI.at[part], R4.at[part], dev(mate=True)))
+
+    def arrive(sets):
+        for st in sets:
+            st.wait_recv()
+
+    def begin(sets):
+        for st in sets:
+            st.start()
 
     def after(came, then):
         for n in range(2):
-            arrive(came[n])
-            start(then[n])
+            came[n].wait_recv()
+            then[n].start()
 
     place[0].wait()
     place[1].wait()
     pl.semaphore_wait(barrier, len(partners))
-    start(by_z[k] for k in (1, 2, 3))
+    begin([by_z[1], by_z[3], by_z[2]])
     begin(first[0])
     place[3].wait()
     place[4].wait()
@@ -142,24 +177,20 @@
     place[2].wait()
     mb[0, 0] = jnp.zeros(mb.shape[2:], jnp.float32)
     mb[0, 0, :, : mask.shape[1]] = mi[...].astype(jnp.float32)
-    start(mask_y)
+    mask_y.start()
     PU[...] = jnp.zeros_like(PU)
     PV[...] = jnp.zeros_like(PV)
     by_z[1].wait_recv()
     begin(first[1])
+    by_z[3].wait_recv()
+    begin(first[3])
+    after(first[0], second[0])
     by_z[2].wait_recv()
     begin(first[2])
-    after(first[0], second[0])
-    by_z[3].wait_recv()
-    begin(first[3])
-    arrive(mask_y)
+    mask_y.wait_recv()
     mask_c.start()
-    after(first[1], second[1])
-    after(first[2], second[2])
-    after(first[3], second[3])
-    mask_c.wait_recv()
-
-    for p in range(2):
+
+    def spread(p):
         zone = zl if p == 0 else 1 - zl
         j = lax.broadcasted_iota(jnp.int32, (128, items), 0)
         l = lax.broadcasted_iota(jnp.int32, (128, items), 1)
@@ -176,6 +207,13 @@
                 Mx[k, p, :, :, pl.ds(cc * items, items)] = dot(put, seen, NN).reshape(
                     16, 8, items
                 )
+
+    mask_c.wait_recv()
+    spread(0)
+    after(first[1], second[1])
+    after(first[3], second[3])
+    spread(1)
+    after(first[2], second[2])
     item_s.wait_recv()
 
     lanes = (slice(0, 128), slice(128, 256))
@@ -201,38 +239,46 @@
                 v = PU[k, :, d, h1] if n else PU[k, d, :, h0]
                 at = (k, n, d - 1)
                 code(v, Q1.at[at], F1.at[at])
-            start(back1[k][n])
+            back1[k][0][n].start()
+            back1[k][1][n].start()
 
     def sum1(k):
         for n in range(2):
-            arrive(back1[k][n])
+            back1[k][0][n].wait_recv()
+            back1[k][1][n].wait_recv()
             own = PU[k, :, 0, h1] if n else PU[k, 0, :, h0]
             for l in lanes:
                 v = own[..., l]
                 for d in (1, 2, 3):
                     v += plain(R1.at[k, n, d - 1], E1.at[k, n, d - 1], l)
                 S1[k, n, :, :, l] = v
-            start(back2[k][n])
+            back2[k][n].start()
 
     def sum2(k):
         for n, h in ((0, h0), (1, h1)):
-            arrive(back2[k][n])
-            S2[k, h] = (S1[k, n, 0] + R2[k, 0, n]) + (R2[k, 1, n] + R2[k, 2, n])
+            back2[k][n].wait_recv()
+            S2[k, h] = (S1[k, n, 0] + R2[k, n, 0]) + (R2[k, n, 1] + R2[k, n, 2])
         if k:
-            back3[k - 1].start()
+            back3.copies[k - 1].start()
 
     tile = items // 2
 
     def step(i, carry):
-        p = lax.div(i, 4)
-        k = lax.rem(i + p, 4)
+        mid, late, last = lax.div(i + 6, 8), lax.div(i + 3, 8), lax.div(i, 7)
+        p = mid - late + last
+        k = i - mid - 2 * late - 4 * last
+
         for n in range(4):
-            @pl.when(i == n)
+            @pl.when(i == (0, 1, 3, 4)[n])
             def _():
-                arrive(second[n][0])
-                arrive(second[n][1])
-
-        @pl.when(i == 4)
+                arrive(second[n])
+
+        @pl.when(i == 1)
+        def _():
+            item_m.wait_recv()
+            item_f.start()
+
+        @pl.when(i == 2)
         def _():
             item_f.wait_recv()
 
@@ -260,52 +306,61 @@
             total = part if total is None else total + part
         PU[k] += total.reshape(4, 4, rows, width)
 
-        @pl.when(i == 2)
+        for n in range(4):
+            @pl.when(i == (7, 2, 5, 6)[n])
+            def _():
+                if n == 0:
+                    sum_s1.start()
+                out1(n)
+
+        @pl.when(i == 5)
         def _():
-            item_m.wait_recv()
-            item_f.start()
-
-        @pl.when(i == 3)
+            sum1(1)
+
+        @pl.when(i == 6)
         def _():
             sum_s0.start()
 
-        for n in range(4):
-            @pl.when(i == 4 + n)
-            def _():
-                if n == 3:
-                    sum_s1.start()
-                out1((n + 1) % 4)
-
         return carry
 
     lax.fori_loop(0, 8, step, 0)
+    sum2(1)
+    sum1(2)
     sum_s1.wait_recv()
     code(PV[2] + RI1[1], QI, FI)
-    start(sum_m)
-    sum1(1)
-    sum1(2)
-    sum2(1)
+    begin(sum_m[:3])
     sum1(3)
+    sum_m[3].start()
     sum2(2)
+    sum_m[4].start()
     sum1(0)
     sum2(3)
+    for cp in gathers:
+        cp.wait_send()
     sum2(0)
-    arrive(back3)
     out = 1.0 / 256.0
-    ou[...] = ((S2[0] + R3[0]) + (R3[1] + R3[2])) * out
     sum_s0.wait_recv()
     arrive(sum_m)
     for l in lanes:
-        oi[:, l] = (PV[0, :, l] + RI1[0, :, l] + plain(R4, E4, l)) * out
-    for cp in made:
+        OI[:, l] = (PV[0, :, l] + RI1[0, :, l] + plain(R4, E4, l)) * out
+    away = [
+        pltpu.make_async_copy(OU, ou, local.at[0]),
+        pltpu.make_async_copy(OI, oi, local.at[1]),
+    ]
+    away[1].start()
+    back3.wait_recv()
+    OU[...] = ((S2[0] + R3[0]) + (R3[1] + R3[2])) * out
+    away[0].start()
+    for cp in made[len(gathers) :]:
         cp.wait_send()
+    for cp in away:
+        cp.wait()
 
 
 def on_device(user_factors, item_factors, user_tangent, item_tangent, block_mask):
     rows, width = user_factors.shape
     items = item_factors.shape[0]
     f32, bf16 = jnp.float32, jnp.bfloat16
-    vmem = pl.BlockSpec(memory_space=pltpu.VMEM)
     scratch = [
         pltpu.VMEM((4, 4, 4, rows, 2 * width), bf16),
         pltpu.VMEM((4, items, 2 * width), bf16),
@@ -319,7 +374,7 @@
         pltpu.VMEM((4, 2, 3, 4, rows // 2, width), jnp.int16),
         pltpu.VMEM((4, 2, 3, 8, 128), f32),
         pltpu.VMEM((4, 2, 4, rows // 2, width), f32),
-        pltpu.VMEM((4, 3, 2, rows // 2, width), f32),
+        pltpu.VMEM((4, 2, 3, rows // 2, width), f32),
         pltpu.VMEM((4, rows, width), f32),
         pltpu.VMEM((3, rows, width), f32),
         pltpu.VMEM((2, items, width), f32),
@@ -327,6 +382,8 @@
         pltpu.VMEM((8, 128), f32),
         pltpu.VMEM((items, width), jnp.int16),
         pltpu.VMEM((8, 128), f32),
+        pltpu.VMEM((rows, width), f32),
+        pltpu.VMEM((items, width), f32),
         pltpu.SemaphoreType.DMA((N_SEM,)),
         pltpu.SemaphoreType.DMA((N_SEM,)),
         pltpu.SemaphoreType.DMA((5,)),
@@ -340,7 +397,7 @@
             jax.ShapeDtypeStruct((items, width), f32),
         ),
         in_specs=[pl.BlockSpec(memory_space=pltpu.HBM)] * 5,
-        out_specs=[vmem] * 2,
+        out_specs=[pl.BlockSpec(memory_space=pl.ANY)] * 2,
         scratch_shapes=scratch,
         compiler_params=pltpu.CompilerParams(
             collective_id=0, has_side_effects=True, vmem_limit_bytes=40 << 20

time: 57.2 us -> 53.9 us (0.942)
  Pallas kernels: 54.7 us -> 51.7 us
    pallas_call x1, Pallas kernels: 54.7 us -> 51.7 us  [on_device(): pl.pallas_call(kernel, out_shape=(jax.ShapeDtypeStruct((rows, width), f32...]
where the time goes in v4:
time: 53.9 us; the launch traced here: 53.8 us
  Pallas kernels  51.7 us (96%)
  local copies, waits for them, and re-layouts  1.41 us (3%)
  between operations  0.64 us (1%)
    pallas_call x1, Pallas kernels, on_device(): pl.pallas_call(kernel, out_shape=(jax.ShapeDtypeStruct((rows, width), f32...  51.7 us
    unnamed x2, local copies, waits for them, and re-layouts  1.41 us

profile of v4, /device:TPU:1, one launch (start us, length us, event | category | flops | bytes accessed | tf_op | source)
XLA Modules:
  0.0 53.8 jit_solution(11953746633985256808)
XLA Ops:
  0.6 51.7 %shard_map.68 = (f32[32,256]{1,0:T(8,128)S(1)}, f32[512,256]{1,0:T(8,128)S(1)}) custom-call(bf16[32,256]{1,0:T(8,128)(2,1)} %uf.1, bf16[32,256]{1,0:T(8,128)(2,1)} %ut.1, bf16[512,256]{1,0:T(8,128)(2,1)} %vf.1, bf16[512,256]{1,0:T(8,128)(2,1)} %vt.1, s32[8,32]{1,0:T(8,128)} %mask.1), custom_call_target="tpu_custom_call" | custom-call | tf_op jit(solution)/shard_map/pallas_call | solution.py:393
  52.4 0.6 %copy.9 = f32[32,256]{1,0:T(8,128)} copy(f32[32,256]{1,0:T(8,128)S(1)} %get-tuple-element.4) | data formatting | bytes 65536
  53.0 0.8 %copy.10 = f32[512,256]{1,0:T(8,128)} copy(f32[512,256]{1,0:T(8,128)S(1)} %get-tuple-element.5) | data formatting | bytes 1048576

commit v5 on v4

--- a/solution.py
+++ b/solution.py
@@ -10,7 +10,7 @@
 TN = (((0,), (0,)), ((), ()))
 NN = (((1,), (0,)), ((), ()))
 ORDER = (0, 1, 2, 3)
-N_SEM = 56
+N_SEM = 57
 
 
 def dot(a, b, dims):
@@ -19,7 +19,7 @@
 
 def kernel(
     uf, ut, vf, vt, mask, ou, oi,
-    G, Z, mi, mb, Mx, PU, PV, Q1, F1, R1, E1, S1, R2, S2, R3, RI1, QI, FI, R4, E4, OU, OI, send, recv, local,
+    G, Z, mi, mb, Mx, PU, PV, Q1, F1, R1, E1, S1, R2, S2, Q3, F3, R3, E3, RI1, QI, FI, R4, E4, OU, OI, send, recv, local,
 ):
     au, ia = lax.axis_index("au"), lax.axis_index("ia")
     y, zl = lax.div(au, 2), lax.rem(au, 2)
@@ -143,7 +143,11 @@
             )
         back1.append((scales, sums))
         back2.append(onward)
-    back3 = Set(R3, [(S2.at[k], R3.at[k - 1], dev(dz=ORDER[k])) for k in (1, 2, 3)])
+    to = [(k - 1, dev(dz=ORDER[k])) for k in (1, 2, 3)]
+    back3 = [
+        Set(E3, [(F3.at[n], E3.at[n], t) for n, t in to]),
+        Set(R3, [(Q3.at[n], R3.at[n], t) for n, t in to]),
+    ]
     sum_s0 = copy(PV.at[1], RI1.at[0], dev(sib=True))
     sum_s1 = copy(PV.at[3], RI1.at[1], dev(sib=True))
     quarter = items // 4
@@ -259,17 +263,45 @@
             back2[k][n].wait_recv()
             S2[k, h] = (S1[k, n, 0] + R2[k, n, 0]) + (R2[k, n, 1] + R2[k, n, 2])
         if k:
-            back3.copies[k - 1].start()
+            code(S2[k], Q3.at[k - 1], F3.at[k - 1])
+            back3[0].copies[k - 1].start()
+            back3[1].copies[k - 1].start()
 
     tile = items // 2
 
-    def step(i, carry):
-        mid, late, last = lax.div(i + 6, 8), lax.div(i + 3, 8), lax.div(i, 7)
-        p = mid - late + last
-        k = i - mid - 2 * late - 4 * last
-
-        for n in range(4):
-            @pl.when(i == (0, 1, 3, 4)[n])
+    def work(k, p):
+        w = G[k].reshape(16 * rows, 2 * width)
+        tiles = 8 if p is None else 4
+
+        def at(q):
+            return (q // 2 if p is None else 2 * p + q // 2), pl.ds((q % 2) * tile, tile)
+
+        def front(q):
+            z = Z[at(q)]
+            return z, dot(w[:, width:], z[:, :width], NT), dot(w, z, NT)
+
+        def rear(q, z, s, t):
+            e = jnp.exp(jnp.abs(s) * (-1.0 / 16.0))
+            r = 1.0 / (1.0 + e)
+            side = q // 4 if p is None else p
+            seen = Mx[k, side, :, :, pl.ds((q % 4) * tile, tile)]
+            cu = (e * r * r * t).reshape(16, rows // 8, 8, tile) * seen[:, None]
+            cu = cu.reshape(16 * rows, tile).astype(jnp.bfloat16)
+            PV[at(q)] += dot(cu, w[:, width:], TN)
+            return dot(cu, z[:, :width], NN)
+
+        total, held = None, front(0)
+        for q in range(tiles):
+            now = held
+            if q < tiles - 1:
+                held = front(q + 1)
+            part = rear(q, *now)
+            total = part if total is None else total + part
+        PU[k] += total.reshape(4, 4, rows, width)
+
+    def early(i, carry):
+        for n in range(2):
+            @pl.when(i == n)
             def _():
                 arrive(second[n])
 
@@ -282,53 +314,35 @@
         def _():
             item_f.wait_recv()
 
-        w = G[k].reshape(16 * rows, 2 * width)
-
-        def front(q):
-            z = Z[2 * p + q // 2, pl.ds((q % 2) * tile, tile)]
-            return z, dot(w[:, width:], z[:, :width], NT), dot(w, z, NT)
-
-        def rear(q, z, s, t):
-            e = jnp.exp(jnp.abs(s) * (-1.0 / 16.0))
-            r = 1.0 / (1.0 + e)
-            seen = Mx[k, p, :, :, pl.ds(q * tile, tile)]
-            cu = (e * r * r * t).reshape(16, rows // 8, 8, tile) * seen[:, None]
-            cu = cu.reshape(16 * rows, tile).astype(jnp.bfloat16)
-            PV[2 * p + q // 2, pl.ds((q % 2) * tile, tile)] += dot(cu, w[:, width:], TN)
-            return dot(cu, z[:, :width], NN)
-
-        total, held = None, front(0)
-        for q in range(4):
-            now = held
-            if q < 3:
-                held = front(q + 1)
-            part = rear(q, *now)
-            total = part if total is None else total + part
-        PU[k] += total.reshape(4, 4, rows, width)
-
-        for n in range(4):
-            @pl.when(i == (7, 2, 5, 6)[n])
+        work(lax.div(i + 1, 2), lax.div(i, 2))
+        return carry
+
+    def late(k, carry):
+        for n in (2, 3):
+            @pl.when(k == n)
             def _():
-                if n == 0:
-                    sum_s1.start()
+                arrive(second[n])
+
+        work(k, None)
+        for n in (2, 3):
+            @pl.when(k == n)
+            def _():
                 out1(n)
-
-        @pl.when(i == 5)
-        def _():
-            sum1(1)
-
-        @pl.when(i == 6)
-        def _():
-            sum_s0.start()
-
         return carry
 
-    lax.fori_loop(0, 8, step, 0)
-    sum2(1)
+    lax.fori_loop(0, 3, early, 0)
+    out1(1)
+    lax.fori_loop(2, 4, late, 0)
+    sum1(1)
+    sum_s0.start()
+    work(0, 1)
+    sum_s1.start()
+    out1(0)
     sum1(2)
     sum_s1.wait_recv()
     code(PV[2] + RI1[1], QI, FI)
     begin(sum_m[:3])
+    sum2(1)
     sum1(3)
     sum_m[3].start()
     sum2(2)
@@ -348,8 +362,12 @@
         pltpu.make_async_copy(OI, oi, local.at[1]),
     ]
     away[1].start()
-    back3.wait_recv()
-    OU[...] = ((S2[0] + R3[0]) + (R3[1] + R3[2])) * out
+    arrive(back3)
+    for l in lanes:
+        v = S2[0, :, l]
+        for n in range(3):
+            v += plain(R3.at[n], E3.at[n], l)
+        OU[:, l] = v * out
     away[0].start()
     for cp in made[len(gathers) :]:
         cp.wait_send()
@@ -376,7 +394,10 @@
         pltpu.VMEM((4, 2, 4, rows // 2, width), f32),
         pltpu.VMEM((4, 2, 3, rows // 2, width), f32),
         pltpu.VMEM((4, rows, width), f32),
-        pltpu.VMEM((3, rows, width), f32),
+        pltpu.VMEM((3, rows, width), jnp.int16),
+        pltpu.VMEM((3, 8, 128), f32),
+        pltpu.VMEM((3, rows, width), jnp.int16),
+        pltpu.VMEM((3, 8, 128), f32),
         pltpu.VMEM((2, items, width), f32),
         pltpu.VMEM((items, width), jnp.int16),
         pltpu.VMEM((8, 128), f32),

time: 53.9 us -> 52.1 us (0.967)
  Pallas kernels: 51.7 us -> 49.9 us
    pallas_call x1, Pallas kernels: 51.7 us -> 49.9 us  [on_device(): pl.pallas_call(kernel, out_shape=(jax.ShapeDtypeStruct((rows, width), f32...]
where the time goes in v5:
time: 52.1 us; the launch traced here: 51.9 us
  Pallas kernels  49.9 us (96%)
  local copies, waits for them, and re-layouts  1.41 us (3%)
  between operations  0.64 us (1%)
    pallas_call x1, Pallas kernels, on_device(): pl.pallas_call(kernel, out_shape=(jax.ShapeDtypeStruct((rows, width), f32...  49.9 us
    unnamed x2, local copies, waits for them, and re-layouts  1.41 us

profile of v5, /device:TPU:1, one launch (start us, length us, event | category | flops | bytes accessed | tf_op | source)
XLA Modules:
  0.0 51.9 jit_solution(14757976904453586246)
XLA Ops:
  0.6 49.9 %shard_map.68 = (f32[32,256]{1,0:T(8,128)S(1)}, f32[512,256]{1,0:T(8,128)S(1)}) custom-call(bf16[32,256]{1,0:T(8,128)(2,1)} %uf.1, bf16[32,256]{1,0:T(8,128)(2,1)} %ut.1, bf16[512,256]{1,0:T(8,128)(2,1)} %vf.1, bf16[512,256]{1,0:T(8,128)(2,1)} %vt.1, s32[8,32]{1,0:T(8,128)} %mask.1), custom_call_target="tpu_custom_call" | custom-call | tf_op jit(solution)/shard_map/pallas_call | solution.py:414
  50.5 0.6 %copy.9 = f32[32,256]{1,0:T(8,128)} copy(f32[32,256]{1,0:T(8,128)S(1)} %get-tuple-element.4) | data formatting | bytes 65536
  51.1 0.8 %copy.10 = f32[512,256]{1,0:T(8,128)} copy(f32[512,256]{1,0:T(8,128)S(1)} %get-tuple-element.5) | data formatting | bytes 1048576

commit v6 on v5

--- a/solution.py
+++ b/solution.py
@@ -10,7 +10,7 @@
 TN = (((0,), (0,)), ((), ()))
 NN = (((1,), (0,)), ((), ()))
 ORDER = (0, 1, 2, 3)
-N_SEM = 57
+N_SEM = 59
 
 
 def dot(a, b, dims):
@@ -122,9 +122,10 @@
         mb.at[0, rest], [(mb.at[0, 0], mb.at[0, 4 - d], dev(dy=d)) for d in far]
     )
     mask_c = copy(mb.at[0], mb.at[1], dev(sib=True))
-    item_m = copy(Z.at[0], Z.at[2], dev(mate=True))
+    h = (pl.ds(0, items // 2), pl.ds(items // 2, items // 2))
+    item_m = [copy(Z.at[0, n], Z.at[2, n], dev(mate=True)) for n in h]
     item_s = copy(Z.at[0], Z.at[1], dev(sib=True))
-    item_f = copy(Z.at[2], Z.at[3], dev(sib=True))
+    item_f = [copy(Z.at[2, n], Z.at[3, n], dev(sib=True)) for n in h]
     gathers = list(made)
     back1, back2 = [], []
     for k in range(4):
@@ -176,7 +177,7 @@
     begin(first[0])
     place[3].wait()
     place[4].wait()
-    item_m.start()
+    begin(item_m)
     item_s.start()
     place[2].wait()
     mb[0, 0] = jnp.zeros(mb.shape[2:], jnp.float32)
@@ -269,12 +270,12 @@
 
     tile = items // 2
 
-    def work(k, p):
+    def work(k, tiles):
         w = G[k].reshape(16 * rows, 2 * width)
-        tiles = 8 if p is None else 4
 
         def at(q):
-            return (q // 2 if p is None else 2 * p + q // 2), pl.ds((q % 2) * tile, tile)
+            side, core, n = tiles[q]
+            return 2 * side + core, pl.ds(n * tile, tile)
 
         def front(q):
             z = Z[at(q)]
@@ -283,38 +284,42 @@
         def rear(q, z, s, t):
             e = jnp.exp(jnp.abs(s) * (-1.0 / 16.0))
             r = 1.0 / (1.0 + e)
-            side = q // 4 if p is None else p
-            seen = Mx[k, side, :, :, pl.ds((q % 4) * tile, tile)]
+            side, core, n = tiles[q]
+            seen = Mx[k, side, :, :, pl.ds((2 * core + n) * tile, tile)]
             cu = (e * r * r * t).reshape(16, rows // 8, 8, tile) * seen[:, None]
             cu = cu.reshape(16 * rows, tile).astype(jnp.bfloat16)
             PV[at(q)] += dot(cu, w[:, width:], TN)
             return dot(cu, z[:, :width], NN)
 
         total, held = None, front(0)
-        for q in range(tiles):
+        for q in range(len(tiles)):
             now = held
-            if q < tiles - 1:
+            if q < len(tiles) - 1:
                 held = front(q + 1)
             part = rear(q, *now)
             total = part if total is None else total + part
         PU[k] += total.reshape(4, 4, rows, width)
 
+    halves = [(core, n) for core in range(2) for n in range(2)]
+
     def early(i, carry):
-        for n in range(2):
-            @pl.when(i == n)
-            def _():
-                arrive(second[n])
+        @pl.when(i == 0)
+        def _():
+            arrive(second[0])
 
         @pl.when(i == 1)
         def _():
-            item_m.wait_recv()
-            item_f.start()
+            item_f[0].wait_recv()
+            work(0, [(1, 0, 0), (1, 1, 0)])
+            arrive(second[1])
+            item_m[1].wait_recv()
+            item_f[1].start()
 
         @pl.when(i == 2)
         def _():
-            item_f.wait_recv()
-
-        work(lax.div(i + 1, 2), lax.div(i, 2))
+            item_f[1].wait_recv()
+
+        work(lax.div(i + 1, 2), [(lax.div(i, 2), *ch) for ch in halves])
         return carry
 
     def late(k, carry):
@@ -323,19 +328,21 @@
             def _():
                 arrive(second[n])
 
-        work(k, None)
+        work(k, [(side, *ch) for side in range(2) for ch in halves])
         for n in (2, 3):
             @pl.when(k == n)
             def _():
                 out1(n)
         return carry
 
+    item_m[0].wait_recv()
+    item_f[0].start()
     lax.fori_loop(0, 3, early, 0)
     out1(1)
     lax.fori_loop(2, 4, late, 0)
     sum1(1)
     sum_s0.start()
-    work(0, 1)
+    work(0, [(1, 1, 1), (1, 0, 1)])
     sum_s1.start()
     out1(0)
     sum1(2)

time: 52.1 us -> 51.1 us (0.981)
  Pallas kernels: 49.9 us -> 48.7 us
    pallas_call x1, Pallas kernels: 49.9 us -> 48.7 us  [on_device(): pl.pallas_call(kernel, out_shape=(jax.ShapeDtypeStruct((rows, width), f32...]
where the time goes in v6:
time: 51.1 us; the launch traced here: 50.7 us
  Pallas kernels  48.7 us (95%)
  local copies, waits for them, and re-layouts  1.41 us (3%)
  between operations  0.64 us (1%)
    pallas_call x1, Pallas kernels, on_device(): pl.pallas_call(kernel, out_shape=(jax.ShapeDtypeStruct((rows, width), f32...  48.7 us
    unnamed x2, local copies, waits for them, and re-layouts  1.41 us

profile of v6, /device:TPU:1, one launch (start us, length us, event | category | flops | bytes accessed | tf_op | source)
XLA Modules:
  0.0 50.7 jit_solution(3321424171608910690)
XLA Ops:
  0.6 48.7 %shard_map.68 = (f32[32,256]{1,0:T(8,128)S(1)}, f32[512,256]{1,0:T(8,128)S(1)}) custom-call(bf16[32,256]{1,0:T(8,128)(2,1)} %uf.1, bf16[32,256]{1,0:T(8,128)(2,1)} %ut.1, bf16[512,256]{1,0:T(8,128)(2,1)} %vf.1, bf16[512,256]{1,0:T(8,128)(2,1)} %vt.1, s32[8,32]{1,0:T(8,128)} %mask.1), custom_call_target="tpu_custom_call" | custom-call | tf_op jit(solution)/shard_map/pallas_call | solution.py:421
  49.3 0.6 %copy.9 = f32[32,256]{1,0:T(8,128)} copy(f32[32,256]{1,0:T(8,128)S(1)} %get-tuple-element.4) | data formatting | bytes 65536
  49.9 0.8 %copy.10 = f32[512,256]{1,0:T(8,128)} copy(f32[512,256]{1,0:T(8,128)S(1)} %get-tuple-element.5) | data formatting | bytes 1048576

commit v7 on v6

--- a/solution.py
+++ b/solution.py
@@ -348,10 +348,9 @@
     sum1(2)
     sum_s1.wait_recv()
     code(PV[2] + RI1[1], QI, FI)
-    begin(sum_m[:3])
+    begin(sum_m[:4])
     sum2(1)
     sum1(3)
-    sum_m[3].start()
     sum2(2)
     sum_m[4].start()
     sum1(0)

time: 51.1 us -> 51.2 us (level)
  no operation moved by 1% of the time
where the time goes in v7:
time: 51.2 us; the launch traced here: 50.8 us
  Pallas kernels  48.8 us (95%)
  local copies, waits for them, and re-layouts  1.41 us (3%)
  between operations  0.64 us (1%)
    pallas_call x1, Pallas kernels, on_device(): pl.pallas_call(kernel, out_shape=(jax.ShapeDtypeStruct((rows, width), f32...  48.8 us
    unnamed x2, local copies, waits for them, and re-layouts  1.41 us

profile of v7, /device:TPU:1, one launch (start us, length us, event | category | flops | bytes accessed | tf_op | source)
XLA Modules:
  0.0 50.8 jit_solution(14918653002738872108)
XLA Ops:
  0.6 48.8 %shard_map.68 = (f32[32,256]{1,0:T(8,128)S(1)}, f32[512,256]{1,0:T(8,128)S(1)}) custom-call(bf16[32,256]{1,0:T(8,128)(2,1)} %uf.1, bf16[32,256]{1,0:T(8,128)(2,1)} %ut.1, bf16[512,256]{1,0:T(8,128)(2,1)} %vf.1, bf16[512,256]{1,0:T(8,128)(2,1)} %vt.1, s32[8,32]{1,0:T(8,128)} %mask.1), custom_call_target="tpu_custom_call" | custom-call | tf_op jit(solution)/shard_map/pallas_call | solution.py:420
  49.4 0.6 %copy.9 = f32[32,256]{1,0:T(8,128)} copy(f32[32,256]{1,0:T(8,128)S(1)} %get-tuple-element.4) | data formatting | bytes 65536
  50.0 0.8 %copy.10 = f32[512,256]{1,0:T(8,128)} copy(f32[512,256]{1,0:T(8,128)S(1)} %get-tuple-element.5) | data formatting | bytes 1048576
